TPU v7x, 32 devices: a whole 2x2x4 slice. The times are simulated.
32 devices in a mesh: tm: 8 (over z, x), col: 4 (over y, core).
Axes of the slice: x: 2, y: 2, z: 4, core: 2. Of those that a mesh axis runs over, the one named last changes fastest.
Arguments:
- jacobians: float32 [96, 512, 512], P('tm'), may hold values from -0.05 to 1.05
- increments: float32 [96, 512], P('tm'), may hold values from -1.5 to 1.5
- initial: float32 [512], P('col'), may hold values from -6 to 6
Outputs:
- states: float32 [96, 512], P('tm', 'col')
All inputs are finite; a program needn't handle non-finite values.
Results may differ from a plain program's by a relative error of at most 0.0003.
Values sent between devices are 32-bit elements; how exact they have to be, the bound alone decides.
No kernel may reach another device: no remote copies, remote signals or barrier semaphores. Data moves between devices by JAX's collectives and lax.ppermute only.
A program may use at most 128 MiB of HBM per device.

v0:
```python
import jax
import jax.numpy as jnp
from jax import lax
from jax.sharding import PartitionSpec as P


def from_behind(block, axis, distance):
    devices = range(lax.axis_size(axis))
    route = [(i - distance, i) for i in devices if i - distance in devices]
    return lax.ppermute(block, axis, route)


def matmul(left, right):
    return jnp.dot(left, right, precision=lax.Precision.HIGHEST, preferred_element_type=jnp.float32)


def body(jacobians, increments, initial):
    part_cols = initial.shape[0]
    column_index = lax.axis_index("col")
    segment_index = lax.axis_index("tm")
    rounds = (lax.axis_size("tm") - 1).bit_length()
    first_col = column_index * part_cols

    def own_cols(matrix):
        return lax.dynamic_slice_in_dim(matrix, first_col, part_cols, matrix.ndim - 1)

    def advance_map(running, inputs):
        step_jac, step_inc = inputs
        return ((matmul(step_jac, running[0]), matmul(step_jac, running[1]) + step_inc), None)

    composed, _ = lax.scan(
        advance_map, (own_cols(jacobians[0]), increments[0]), (jacobians[1:], increments[1:])
    )
    acc_map, acc_off = composed
    for level_index in range(rounds):
        distance = 1 << level_index
        recv_map, recv_off = from_behind((acc_map, acc_off), "tm", distance)

        def fold_columns(running, col_block, first_row, recv_map=recv_map, recv_off=recv_off):
            return (matmul(col_block, recv_map), running[1] + matmul(col_block, recv_off))

        new_map, new_off = fold_columns(
            (jnp.zeros_like(acc_map), acc_off),
            lax.all_gather(acc_map, "col", axis=1, tiled=True),
            jnp.int32(0),
        )
        active = segment_index >= distance
        acc_map = jnp.where(active, new_map, acc_map)
        acc_off = jnp.where(active, new_off, acc_off)
    end_part = matmul(acc_map, initial)
    end_mine = lax.psum_scatter(end_part, "col", scatter_dimension=0, tiled=True) + own_cols(
        acc_off
    )
    handed = from_behind(end_mine, "tm", 1)
    start_mine = jnp.where(segment_index == 0, initial, handed)
    start_full = lax.all_gather(start_mine, "col", axis=0, tiled=True)

    def advance_state(current, inputs):
        step_jac, step_inc = inputs
        following = matmul(step_jac, current) + step_inc
        return (following, own_cols(following))

    _, leading = lax.scan(advance_state, start_full, (jacobians[:-1], increments[:-1]))
    return jnp.concatenate([leading, end_mine[None, :]], axis=0)


def solution(mesh):
    return jax.shard_map(
        body,
        mesh=mesh,
        in_specs=(P("tm", None, None), P("tm", None), P("col")),
        out_specs=P("tm", "col"),
        check_vma=False,
    )
```

profile of v0, /device:TPU:24, one launch (start us, length us, event | category | flops | bytes accessed | tf_op | source)
XLA Modules:
  0.0 202.2 jit_solution(5260583161376502509)
XLA Ops:
  6.5 17.6 %fusion.15 = (f32[11,512,512]{2,1,0:T(8,128)}, f32[11,512,512]{2,1,0:T(8,128)}) fusion(f32[12,512,512]{2,1,0:T(8,128)} %param.7), kind=kLoop, calls=%fused_computation.28 | loop fusion | bytes 46137344 | tf_op jit(solution)/shard_map/slice | solution.py:63
  24.2 49.5 %while.26 = (s32[]{:T(128)}, f32[512,128]{1,0:T(8,128)S(1)}, f32[512]{0:T(512)S(1)}, f32[11,512,512]{2,1,0:T(8,128)}, f32[11,512]{1,0:T(8,128)S(1)}, /*index=5*/s32[]{:T(128)}) while((s32[]{:T(128)}, f32[512,128]{1,0:T(8,128)S(1)}, f32[512]{0:T(512)S(1)}, f32[11,512,512]{2,1,0:T(8,128)}, f32[11,512]{1,0:T(8,128)S(1)}, ...), condition=%wide.region_1.2_spmd, body=%wide.region_0.1_spmd.sunk | while | flops 405799424 | bytes 3161161 | solution.py:31
  26.5 2.2 %fusion.49 = f32[512,128]{1,0:T(8,128)S(1)} fusion(f32[512,128]{1,0:T(8,128)S(1)} %copy.24, f32[11,512,512]{2,1,0:T(8,128)} %get-tuple-element.219, s32[]{:T(128)} %get-tuple-element.210), kind=kOutput, calls=%fused_computation.2.clone.1 | convolution fusion | flops 402653184 | bytes 1573376 | tf_op jit(solution)/shard_map/while/body/eval_jaxpr/dot_general | solution.py:14
  35.5 2.2 %fusion.49 = f32[512,128]{1,0:T(8,128)S(1)} fusion(f32[512,128]{1,0:T(8,128)S(1)} %copy.24, f32[11,512,512]{2,1,0:T(8,128)} %get-tuple-element.219, s32[]{:T(128)} %get-tuple-element.210), kind=kOutput, calls=%fused_computation.2.clone.1 | convolution fusion | flops 402653184 | bytes 1573376 | tf_op jit(solution)/shard_map/while/body/eval_jaxpr/dot_general | solution.py:14
  67.0 2.2 %fusion.49 = f32[512,128]{1,0:T(8,128)S(1)} fusion(f32[512,128]{1,0:T(8,128)S(1)} %copy.24, f32[11,512,512]{2,1,0:T(8,128)} %get-tuple-element.219, s32[]{:T(128)} %get-tuple-element.210), kind=kOutput, calls=%fused_computation.2.clone.1 | convolution fusion | flops 402653184 | bytes 1573376 | tf_op jit(solution)/shard_map/while/body/eval_jaxpr/dot_general | solution.py:14
  74.5 3.4 %collective-permute-start = (f32[512,128]{1,0:T(8,128)}, f32[512,128]{1,0:T(8,128)S(1)}, u32[]{:S(2)}, u32[]{:S(2)}) collective-permute-start(f32[512,128]{1,0:T(8,128)} %copy-done), channel_id=1, source_target_pairs={{0,4},{4,8},{8,12},{12,16},{16,20},{20,24},{24,28},{1,5},{5,9},{9,... | collective-permute-start | bytes 786440 | tf_op jit(solution)/shard_map/ppermute | solution.py:10
  77.9 7.6 %collective-permute-done = f32[512,128]{1,0:T(8,128)S(1)} collective-permute-done((f32[512,128]{1,0:T(8,128)}, f32[512,128]{1,0:T(8,128)S(1)}, u32[]{:S(2)}, u32[]{:S(2)}) %collective-permute-start) | collective-permute-done | bytes 262176 | tf_op jit(solution)/shard_map/ppermute | solution.py:10
  85.6 6.8 %all-gather.5.cloned.1.call-done = f32[512,512]{1,0:T(8,128)} async-done(((f32[512,128]{1,0:T(8,128)}), f32[512,512]{1,0:T(8,128)}) %all-gather.5.cloned.1.call-update) | async-done | bytes 1048592 | tf_op jit(solution)/shard_map/all_gather | solution.py:44
  92.4 2.9 %convolution_select_fusion.2 = f32[512,128]{1,0:T(8,128)} fusion(f32[512,128]{1,0:T(8,128)} %copy-done, f32[512,512]{1,0:T(8,128)} %all-gather.5.cloned.1.call-done, f32[512,128]{1,0:T(8,128)S(1)} %collective-permute-done, pred[]{:T(512)S(6)} %ge.11), kind=kOutput, calls=%fused_computation.17 | convolution fusion | flops 402718720 | bytes 1835009 | tf_op jit(solution)/shard_map/dot_general | solution.py:14
  96.7 9.2 %collective-permute-done.1 = f32[512,128]{1,0:T(8,128)S(1)} collective-permute-done((f32[512,128]{1,0:T(8,128)}, f32[512,128]{1,0:T(8,128)S(1)}, u32[]{:S(2)}, u32[]{:S(2)}) %collective-permute-start.1) | collective-permute-done | bytes 262176 | tf_op jit(solution)/shard_map/ppermute | solution.py:10
  106.0 6.4 %all-gather.7.cloned.1.call-done = f32[512,512]{1,0:T(8,128)} async-done(((f32[512,128]{1,0:T(8,128)}), f32[512,512]{1,0:T(8,128)}) %all-gather.7.cloned.1.call-update) | async-done | bytes 1048592 | tf_op jit(solution)/shard_map/all_gather | solution.py:44
  112.3 2.9 %convolution_select_fusion.1 = f32[512,128]{1,0:T(8,128)} fusion(f32[512,128]{1,0:T(8,128)} %convolution_select_fusion.2, f32[512,512]{1,0:T(8,128)} %all-gather.7.cloned.1.call-done, f32[512,128]{1,0:T(8,128)S(1)} %collective-permute-done.1, pred[]{:T(512)S(6)} %ge.10), kind=kOutput, calls=%fused_computation.16 | convolution fusion | flops 402718720 | bytes 1835009 | tf_op jit(solution)/shard_map/dot_general | solution.py:14
  115.3 3.4 %collective-permute-start.3 = (f32[512]{0:T(512)S(1)}, f32[512]{0:T(512)S(1)}, u32[]{:S(2)}, u32[]{:S(2)}) collective-permute-start(f32[512]{0:T(512)S(1)} %get-tuple-element.108), channel_id=1, source_target_pairs={{0,4},{4,8},{8,12},{12,16},{16,20},{20,24},{24,28},{1,5},{5,9},{9,... | collective-permute-start | bytes 6152 | tf_op jit(solution)/shard_map/ppermute | solution.py:10
  118.7 3.0 %collective-permute-done.3 = f32[512]{0:T(512)S(1)} collective-permute-done((f32[512]{0:T(512)S(1)}, f32[512]{0:T(512)S(1)}, u32[]{:S(2)}, u32[]{:S(2)}) %collective-permute-start.3) | collective-permute-done | bytes 2080 | tf_op jit(solution)/shard_map/ppermute | solution.py:10
  121.6 2.2 %fusion.17 = f32[1,512]{1,0:T(1,128)S(1)} fusion(f32[512,512]{1,0:T(8,128)} %all-gather.5.cloned.1.call-done, f32[512,1]{0,1:T(1,128)S(1)} %bitcast.89), kind=kOutput, calls=%fused_computation.30 | convolution fusion | flops 3145728 | bytes 1052672 | tf_op jit(solution)/shard_map/dot_general | solution.py:14
  125.2 4.2 %collective-permute-done.4 = f32[512]{0:T(512)S(1)} collective-permute-done((f32[512]{0:T(512)S(1)}, f32[512]{0:T(512)S(1)}, u32[]{:S(2)}, u32[]{:S(2)}) %collective-permute-start.4) | collective-permute-done | bytes 2080 | tf_op jit(solution)/shard_map/ppermute | solution.py:10
  135.5 2.5 %collective-permute-done.5 = f32[512]{0:T(512)S(1)} collective-permute-done((f32[512]{0:T(512)S(1)}, f32[512]{0:T(512)S(1)}, u32[]{:S(2)}, u32[]{:S(2)}) %collective-permute-start.5) | collective-permute-done | bytes 2080 | tf_op jit(solution)/shard_map/ppermute | solution.py:10
  140.2 9.1 %collective-permute-done.2 = f32[512,128]{1,0:T(8,128)S(1)} collective-permute-done((f32[512,128]{1,0:T(8,128)}, f32[512,128]{1,0:T(8,128)S(1)}, u32[]{:S(2)}, u32[]{:S(2)}) %collective-permute-start.2) | collective-permute-done | bytes 262176 | tf_op jit(solution)/shard_map/ppermute | solution.py:10
  149.4 2.2 %convolution_select_fusion = f32[512,128]{1,0:T(8,128)S(1)} fusion(f32[512,128]{1,0:T(8,128)} %convolution_select_fusion.1, f32[512,512]{1,0:T(8,128)} %all-gather.9.cloned.1.call-done, f32[512,128]{1,0:T(8,128)S(1)} %collective-permute-done.2, pred[]{:T(512)S(6)} %ge.9), kind=kOutput, calls=%fused_computation.15 | convolution fusion | flops 402718720 | bytes 1835009 | tf_op jit(solution)/shard_map/dot_general | solution.py:14
  151.9 5.9 %all-reduce = f32[512]{0:T(512)S(1)} all-reduce(f32[512]{0:T(512)S(1)} %bitcast.87), channel_id=2, replica_groups=mesh['tm'=8,'col'=4] {'col'}, use_global_device_ids=true, to_apply=%region_2.3.clone | all-reduce | flops 512 | bytes 4096
  157.9 2.4 %collective-permute-start.6 = (f32[128]{0:T(128)S(1)}, f32[128]{0:T(128)S(1)}, u32[]{:S(2)}, u32[]{:S(2)}) collective-permute-start(f32[128]{0:T(128)S(1)} %dynamic-slice_add_fusion), channel_id=1, source_target_pairs={{0,4},{4,8},{8,12},{12,16},{16,20},{20,24},{24,28},{1,5},{5,9},{9,... | collective-permute-start | bytes 1544 | tf_op jit(solution)/shard_map/ppermute | solution.py:10
  160.3 3.9 %collective-permute-done.6 = f32[128]{0:T(128)S(1)} collective-permute-done((f32[128]{0:T(128)S(1)}, f32[128]{0:T(128)S(1)}, u32[]{:S(2)}, u32[]{:S(2)}) %collective-permute-start.6) | collective-permute-done | bytes 544 | tf_op jit(solution)/shard_map/ppermute | solution.py:10
  164.2 5.0 %all-gather = f32[4,1,128]{2,1,0:T(1,128)S(1)} all-gather(f32[1,1,128]{2,1,0:T(1,128)S(1)} %fusion.12), channel_id=1, replica_groups=mesh['tm'=8,'col'=4] {'col'}, dimensions={0}, use_global_device_ids=true | all-gather | bytes 2560 | tf_op jit(solution)/shard_map/all_gather | solution.py:56
  169.3 25.8 %while.27 = (s32[]{:T(128)}, f32[512]{0:T(512)S(1)}, f32[11,128]{1,0:T(8,128)S(1)}, f32[11,512,512]{2,1,0:T(8,128)}, f32[11,512]{1,0:T(8,128)S(1)}, /*index=5*/s32[]{:T(128)}, s32[]{:T(128)}, s32[]{:T(128)}) while((s32[]{:T(128)}, f32[512]{0:T(512)S(1)}, f32[11,128]{1,0:T(8,128)S(1)}, f32[11,512,512]{2,1,0:T(8,128)}, f32[11,512]{1,0:T(8,128)S(1)}, ...), condition=%wide.region_4.5_spmd, body=%wide.region_3.4_spmd.sunk | while | flops 3146242 | bytes 1065569 | solution.py:63
  (143 shorter events, 80.1 us)
Async XLA Ops:
  6.5 85.9 %all-gather.5.cloned.1.call-start = ((), (), s32[]{:S(2)}) async-start(), calls=%async_computation | async-start | bytes 1310720 | tf_op jit(solution)/shard_map/all_gather | solution.py:44
  6.5 17.6 %copy-start.1 = (f32[12,512]{1,0:T(8,128)S(1)}, f32[12,512]{1,0:T(8,128)}, u32[]{:S(2)}) copy-start(f32[12,512]{1,0:T(8,128)} %param.8) | copy-start | bytes 73732
  6.5 17.6 %slice-start = ((f32[12,512,512]{2,1,0:T(8,128)}), f32[1,512,512]{2,1,0:T(8,128)S(1)}, s32[]{:S(2)}) async-start(f32[12,512,512]{2,1,0:T(8,128)} %param.7), calls=%async_computation.3 | async-start | bytes 2097152 | tf_op jit(solution)/shard_map/slice | solution.py:32
  6.5 17.7 %slice-start.1 = ((f32[12,512]{1,0:T(8,128)}), f32[1,512]{1,0:T(1,128)S(1)}, s32[]{:S(2)}) async-start(f32[12,512]{1,0:T(8,128)} %param.8), calls=%async_computation.4 | async-start | bytes 4096 | tf_op jit(solution)/shard_map/slice | solution.py:32
  24.1 108.8 %copy-start.3 = (u32[32]{0:T(128)S(1)}, u32[32]{0:T(128)}, u32[]{:S(2)}) copy-start(u32[32]{0:T(128)} %constant.58) | copy-start | bytes 388
  24.2 127.4 %copy-start.2 = (f32[128]{0:T(128)S(1)}, f32[128]{0:T(128)}, u32[]{:S(2)}) copy-start(f32[128]{0:T(128)} %param.9) | copy-start | bytes 1540
  73.7 0.7 copy-start
  74.5 37.9 %all-gather.7.cloned.1.call-start = ((), (), s32[]{:S(2)}) async-start(), calls=%async_computation.1 | async-start | bytes 1310720 | tf_op jit(solution)/shard_map/all_gather | solution.py:44
  74.5 11.1 %collective-permute-start = (f32[512,128]{1,0:T(8,128)}, f32[512,128]{1,0:T(8,128)S(1)}, u32[]{:S(2)}, u32[]{:S(2)}) collective-permute-start(f32[512,128]{1,0:T(8,128)} %copy-done), channel_id=1, source_target_pairs={{0,4},{4,8},{8,12},{12,16},{16,20},{20,24},{24,28},{1,5},{5,9},{9,... | collective-permute-start | bytes 786440 | tf_op jit(solution)/shard_map/ppermute | solution.py:10
  95.4 42.6 %all-gather.9.cloned.1.call-start = ((), (), s32[]{:S(2)}) async-start(), calls=%async_computation.2 | async-start | bytes 1310720 | tf_op jit(solution)/shard_map/all_gather | solution.py:44
  95.4 10.6 %collective-permute-start.1 = (f32[512,128]{1,0:T(8,128)}, f32[512,128]{1,0:T(8,128)S(1)}, u32[]{:S(2)}, u32[]{:S(2)}) collective-permute-start(f32[512,128]{1,0:T(8,128)} %convolution_select_fusion.2), channel_id=1, source_target_pairs={{0,8},{4,12},{8,16},{12,20},{16,24},{20,28},{1,9},{5,13},{9,17},{1... | collective-permute-start | bytes 786440 | tf_op jit(solution)/shard_map/ppermute | solution.py:10
  115.3 6.4 %collective-permute-start.3 = (f32[512]{0:T(512)S(1)}, f32[512]{0:T(512)S(1)}, u32[]{:S(2)}, u32[]{:S(2)}) collective-permute-start(f32[512]{0:T(512)S(1)} %get-tuple-element.108), channel_id=1, source_target_pairs={{0,4},{4,8},{8,12},{12,16},{16,20},{20,24},{24,28},{1,5},{5,9},{9,... | collective-permute-start | bytes 6152 | tf_op jit(solution)/shard_map/ppermute | solution.py:10
  123.9 5.5 %collective-permute-start.4 = (f32[512]{0:T(512)S(1)}, f32[512]{0:T(512)S(1)}, u32[]{:S(2)}, u32[]{:S(2)}) collective-permute-start(f32[512]{0:T(512)S(1)} %add_select_fusion.2), channel_id=1, source_target_pairs={{0,8},{4,12},{8,16},{12,20},{16,24},{20,28},{1,9},{5,13},{9,17},{1... | collective-permute-start | bytes 6152 | tf_op jit(solution)/shard_map/ppermute | solution.py:10
  131.6 6.4 %collective-permute-start.5 = (f32[512]{0:T(512)S(1)}, f32[512]{0:T(512)S(1)}, u32[]{:S(2)}, u32[]{:S(2)}) collective-permute-start(f32[512]{0:T(512)S(1)} %add_select_fusion.1), channel_id=1, source_target_pairs={{0,16},{4,20},{8,24},{12,28},{1,17},{5,21},{9,25},{13,29},{2,18},{... | collective-permute-start | bytes 6152 | tf_op jit(solution)/shard_map/ppermute | solution.py:10
  134.2 15.2 %collective-permute-start.2 = (f32[512,128]{1,0:T(8,128)}, f32[512,128]{1,0:T(8,128)S(1)}, u32[]{:S(2)}, u32[]{:S(2)}) collective-permute-start(f32[512,128]{1,0:T(8,128)} %convolution_select_fusion.1), channel_id=1, source_target_pairs={{0,16},{4,20},{8,24},{12,28},{1,17},{5,21},{9,25},{13,29},{2,18},{... | collective-permute-start | bytes 786440 | tf_op jit(solution)/shard_map/ppermute | solution.py:10
  157.9 6.4 %collective-permute-start.6 = (f32[128]{0:T(128)S(1)}, f32[128]{0:T(128)S(1)}, u32[]{:S(2)}, u32[]{:S(2)}) collective-permute-start(f32[128]{0:T(128)S(1)} %dynamic-slice_add_fusion), channel_id=1, source_target_pairs={{0,4},{4,8},{8,12},{12,16},{16,20},{20,24},{24,28},{1,5},{5,9},{9,... | collective-permute-start | bytes 1544 | tf_op jit(solution)/shard_map/ppermute | solution.py:10
Sparse Core Ops, SparseCore 0:
  74.6 17.7 all-gather.4
  95.5 16.8 all-gather.6
  115.4 16.8 all-gather.8
where the time goes:
time: 205 us; the launch traced here: 202 us
  matrix products  87.8 us (43%)
  waiting for transfers between devices  52.9 us (26%)
  local copies, waits for them, and re-layouts  20.7 us (10%)
  starting transfers between devices  14.5 us (7%)
  between operations  14 us (7%)
  blocking collectives  10.9 us (5%)
    dot_general x40, matrix products, matmul(): jnp.dot(left, right, precision=lax.Precision.HIGHEST, preferred_element_t...  87.8 us
    ppermute x7, waiting for transfers between devices, from_behind(): return lax.ppermute(block, axis, route)  39.6 us
    slice x1, local copies, waits for them, and re-layouts, body(): jacobians[:-1]  17.6 us
    ppermute x7, starting transfers between devices, from_behind(): return lax.ppermute(block, axis, route)  14.4 us
    all_gather x3, waiting for transfers between devices, body(): lax.all_gather(acc_map, 'col', axis=1, tiled=True)  13.2 us
    unnamed x1, blocking collectives  5.88 us
    all_gather x1, blocking collectives, body(): start_full = lax.all_gather(start_mine, 'col', axis=0, tiled=True)  5.05 us
  transfers between devices with their start and end apart: 10, of which 9 were waited for; matrix products, arithmetic and copies ran while one was open for 4% of the time, Pallas kernels for 0%

commit v1 on v0

v1 whole, which is shorter than its diff:
```python
import functools

import jax
import jax.numpy as jnp
from jax import lax
from jax.experimental import pallas as pl
from jax.experimental.pallas import tpu as pltpu
from jax.sharding import PartitionSpec as P

AXES = ("tm", "col")
LANES = 128
DIRECT = 3
VMEM = pl.BlockSpec(memory_space=pltpu.VMEM)


def swap_pairs(size, moved):
    target = dict(moved)
    for device in range(size):
        partner = device ^ 1
        if device not in target and partner < size and partner not in target:
            target[device] = partner
            target[partner] = device
    return sorted(target.items())


def hop(block, segment):
    segments, parts = lax.axis_size("tm"), lax.axis_size("col")
    moved = {}
    for part in range(parts):
        here = segment * parts + part
        there = here + parts
        moved[here] = there
        moved[there] = here
    return lax.ppermute(block, AXES, swap_pairs(segments * parts, moved))


def gather_parts(own):
    parts = lax.axis_size("col")
    index = lax.axis_index("col")
    width = own.shape[1]
    full = lax.dynamic_update_slice(
        jnp.zeros((1, width * parts), own.dtype), own, (jnp.int32(0), index * width)
    )
    bit = 1
    while bit < parts:
        route = [(i, i ^ bit) for i in range(parts)]
        full = full + lax.ppermute(full, "col", route)
        bit *= 2
    return full


def apply_map(rows_of, offset, vector):
    order = vector.shape[1]
    diagonal = lax.broadcasted_iota(jnp.int32, (LANES, LANES), 0) == lax.broadcasted_iota(
        jnp.int32, (LANES, LANES), 1
    )
    pieces = []
    for top in range(0, order, LANES):
        total = None
        for left in range(0, order, LANES):
            term = rows_of(top, left) * vector[:, left : left + LANES]
            total = term if total is None else total + term
        column = jnp.sum(total, axis=1, keepdims=True)
        pieces.append(jnp.sum(jnp.where(diagonal, column, 0.0), axis=0, keepdims=True))
    return jnp.concatenate(pieces, axis=1) + offset


def step(jac, inc, t, vector):
    return apply_map(
        lambda top, left: jac[t, pl.ds(top, LANES), pl.ds(left, LANES)],
        inc[pl.ds(t, 1), :],
        vector,
    )


def run_segment(jac, inc, vector):
    return lax.fori_loop(0, jac.shape[0], lambda t, v: step(jac, inc, t, v), vector)


def halves(value):
    high = value.astype(jnp.bfloat16)
    return high, (value - high.astype(jnp.float32)).astype(jnp.bfloat16)


def product(left, right):
    left_high, left_low = halves(left)
    right_high, right_low = halves(right)

    def dot(a, b):
        return jnp.dot(a, b, preferred_element_type=jnp.float32)

    return dot(left_high, right_high) + (dot(left_high, right_low) + dot(left_low, right_high))


def compose_kernel(jac, inc, start, out, whole, offset):
    segment = lax.axis_index("tm")
    steps = jac.shape[0]

    @pl.when(segment == 0)
    def _():
        out[...] = run_segment(jac, inc, start[...])

    @pl.when(segment >= DIRECT)
    def _():
        offset[...] = run_segment(jac, inc, jnp.zeros_like(start))
        whole[...] = jac[0]

        def body(t, carry):
            whole[...] = product(jac[t], whole[...])
            return carry

        lax.fori_loop(1, steps, body, 0)


def hop_kernel(k, jac, inc, whole, offset, received, kept, out, start):
    here = lax.axis_index("tm") == k

    @pl.when(here)
    def _():
        vector = received[...]
        start[...] = vector
        if k < DIRECT:
            out[...] = run_segment(jac, inc, vector)
        else:
            out[...] = apply_map(
                lambda top, left: whole[pl.ds(top, LANES), pl.ds(left, LANES)],
                offset[...],
                vector,
            )

    @pl.when(jnp.logical_not(here))
    def _():
        start[...] = kept[...]
        out[...] = kept[...]


def states_kernel(last, jac, inc, received, kept, out):
    index = lax.axis_index("tm")
    part = out.shape[1]
    first = pl.multiple_of(lax.axis_index("col") * part, part)
    vector = jnp.where(index == last, received[...], kept[...])

    def body(t, v):
        v = step(jac, inc, t, v)
        hidden = lax.broadcasted_iota(jnp.int32, v.shape, 1)
        own = v[:, 0:part]
        for other in range(1, v.shape[1] // part):
            own = jnp.where(first == other * part, v[:, other * part : (other + 1) * part], own)
        out[pl.ds(t, 1), :] = own
        return v

    lax.fori_loop(0, jac.shape[0], body, vector)


def call(kernel, outs, *args, limit=8 << 20):
    return pl.pallas_call(
        kernel,
        out_shape=outs,
        in_specs=[VMEM] * len(args),
        out_specs=jax.tree.map(lambda _: VMEM, outs),
        compiler_params=pltpu.CompilerParams(vmem_limit_bytes=limit),
    )(*args)


def body(jacobians, increments, initial):
    segments = lax.axis_size("tm")
    steps, order, _ = jacobians.shape
    jac = pltpu.with_memory_space_constraint(jacobians, pltpu.VMEM)
    row = pltpu.VMEM((1, order), jnp.float32)
    start0 = gather_parts(initial[None, :])
    out, whole, offset = call(
        compose_kernel,
        (row, pltpu.VMEM((order, order), jnp.float32), row),
        jac,
        increments,
        start0,
        limit=24 << 20,
    )
    kept = start0
    for k in range(1, segments):
        received = hop(out, k - 1)
        if k == segments - 1:
            break
        out, kept = call(
            functools.partial(hop_kernel, k), (row, row), jac, increments, whole, offset, received, kept
        )
    return call(
        functools.partial(states_kernel, segments - 1),
        jax.ShapeDtypeStruct((steps, initial.shape[0]), jnp.float32),
        jac,
        increments,
        received,
        kept,
    )


def solution(mesh):
    return jax.shard_map(
        body,
        mesh=mesh,
        in_specs=(P("tm", None, None), P("tm", None), P("col")),
        out_specs=P("tm", "col"),
        check_vma=False,
    )
```

time: 205 us -> 45.7 us (0.22); the launches traced: 202 us -> 45.5 us
  matrix products: 87.8 us -> 0 us
  waiting for transfers between devices: 52.9 us -> 13.5 us
  Pallas kernels: 0 us -> 15.7 us
  local copies, waits for them, and re-layouts: 20.7 us -> 6 us
  between operations: 14 us -> 0.05 us
  blocking collectives: 10.9 us -> 0 us
  starting transfers between devices: 14.5 us -> 9.56 us
    dot_general x40 -> x0, matrix products: 87.8 us -> none  [matmul(): jnp.dot(left, right, precision=lax.Precision.HIGHEST, preferred_element_t...]
    ppermute x7 -> x9, waiting for transfers between devices: 39.6 us -> 13.5 us  [the longest x7 10.3 us: hop(): return lax.ppermute(block, AXES, swap_pairs(segments * parts, moved))]
    slice x6 -> x0, local copies, waits for them, and re-layouts: 17.6 us -> none  [the longest x1 17.6 us: body(): jacobians[:-1]]
    pallas_call x0 -> x8, Pallas kernels: none -> 15.7 us  [call(): pl.pallas_call(kernel, out_shape=outs, in_specs=[VMEM] * len(args), out_s...]
    all_gather x3 -> x0, waiting for transfers between devices: 13.2 us -> none  [body(): lax.all_gather(acc_map, 'col', axis=1, tiled=True)]
    unnamed x1 -> x0, blocking collectives: 5.88 us -> none
    all_gather x1 -> x0, blocking collectives: 5.05 us -> none  [body(): start_full = lax.all_gather(start_mine, 'col', axis=0, tiled=True)]
    ppermute x7 -> x9, starting transfers between devices: 14.4 us -> 9.56 us  [the longest x7 8.04 us: hop(): return lax.ppermute(block, AXES, swap_pairs(segments * parts, moved))]
  transfers between devices with their start and end apart: 10 -> 9, of which waited for: 9 -> 9; matrix products, arithmetic and copies ran while one was open for 4% -> 0% of each run, Pallas kernels for 0% -> 0%
where the time goes in v1:
time: 45.7 us; the launch traced here: 45.5 us
  Pallas kernels  15.7 us (34%)
  waiting for transfers between devices  13.5 us (30%)
  starting transfers between devices  9.56 us (21%)
  local copies, waits for them, and re-layouts  6 us (13%)
  other arithmetic  0.67 us (1%)
    pallas_call x8, Pallas kernels, call(): pl.pallas_call(kernel, out_shape=outs, in_specs=[VMEM] * len(args), out_s...  15.7 us
    ppermute x7, waiting for transfers between devices, hop(): return lax.ppermute(block, AXES, swap_pairs(segments * parts, moved))  10.3 us
    ppermute x7, starting transfers between devices, hop(): return lax.ppermute(block, AXES, swap_pairs(segments * parts, moved))  8.04 us
    unnamed x4, local copies, waits for them, and re-layouts  5.33 us
    ppermute x2, waiting for transfers between devices, gather_parts(): full = full + lax.ppermute(full, 'col', route)  3.23 us
    ppermute x2, starting transfers between devices, gather_parts(): full = full + lax.ppermute(full, 'col', route)  1.52 us
  transfers between devices with their start and end apart: 9, of which 9 were waited for; matrix products, arithmetic and copies ran while one was open for 0% of the time, Pallas kernels for 0%

profile of v1, /device:TPU:24, one launch (start us, length us, event | category | flops | bytes accessed | tf_op | source)
XLA Modules:
  0.0 45.5 jit_solution(15306752799753333859)
XLA Ops:
  0.0 0.7 %constant_dynamic-update-slice_fusion.1 = f32[1,512]{1,0:T(1,128)S(1)} fusion(f32[1,512]{1,0:T(1,128)S(1)} %broadcast_in_dim.6, s32[]{:T(128)S(6)} %select_n.3, f32[128]{0:T(128)} %param.5), kind=kLoop, calls=%fused_computation.2 | loop fusion | bytes 1028 | tf_op jit(solution)/shard_map/dynamic_update_slice | solution.py:41
  0.7 1.2 %collective-permute-done = f32[1,512]{1,0:T(1,128)S(1)} collective-permute-done((f32[1,512]{1,0:T(1,128)S(1)}, f32[1,512]{1,0:T(1,128)S(1)}, u32[]{:S(2)}, u32[]{:S(2)}) %collective-permute-start) | collective-permute-done | bytes 2080 | tf_op jit(solution)/shard_map/ppermute | solution.py:47
  1.8 0.7 %constant_dynamic-update-slice_fusion = f32[1,512]{1,0:T(1,128)S(1)} fusion(f32[1,512]{1,0:T(1,128)S(1)} %collective-permute-done, s32[]{:T(128)S(6)} %select_n.3, f32[128]{0:T(128)} %param.5), kind=kLoop, calls=%fused_computation | loop fusion | flops 128 | bytes 1540 | tf_op jit(solution)/shard_map/add | solution.py:47
  2.5 1.5 %collective-permute-start.1 = (f32[1,512]{1,0:T(1,128)S(1)}, f32[1,512]{1,0:T(1,128)S(1)}, u32[]{:S(2)}, u32[]{:S(2)}) collective-permute-start(f32[1,512]{1,0:T(1,128)S(1)} %constant_dynamic-update-slice_fusion), channel_id=1, source_target_pairs={{0,2},{1,3},{2,0},{3,1},{4,6},{5,7},{6,4},{7,5},{8,10},{9,11},{10,... | collective-permute-start | bytes 6152 | tf_op jit(solution)/shard_map/ppermute | solution.py:47
  4.0 2.1 %collective-permute-done.1 = f32[1,512]{1,0:T(1,128)S(1)} collective-permute-done((f32[1,512]{1,0:T(1,128)S(1)}, f32[1,512]{1,0:T(1,128)S(1)}, u32[]{:S(2)}, u32[]{:S(2)}) %collective-permute-start.1) | collective-permute-done | bytes 2080 | tf_op jit(solution)/shard_map/ppermute | solution.py:47
  6.1 4.6 %copy-done = f32[12,512,512]{2,1,0:T(8,128)S(1)} copy-done((f32[12,512,512]{2,1,0:T(8,128)S(1)}, f32[12,512,512]{2,1,0:T(8,128)}, u32[]{:S(2)}) %copy-start) | copy-done | bytes 12582936
  10.7 0.8 %copy-done.1 = f32[12,512]{1,0:T(8,128)S(1)} copy-done((f32[12,512]{1,0:T(8,128)S(1)}, f32[12,512]{1,0:T(8,128)}, u32[]{:S(2)}) %copy-start.1) | copy-done | bytes 24600
  11.4 13.0 %shard_map.37 = (f32[1,512]{1,0:T(1,128)S(1)}, f32[512,512]{1,0:T(8,128)S(1)}, f32[1,512]{1,0:T(1,128)S(1)}) custom-call(f32[12,512,512]{2,1,0:T(8,128)S(1)} %copy-done, f32[12,512]{1,0:T(8,128)S(1)} %copy-done.1, f32[1,512]{1,0:T(1,128)S(1)} %add.12.start.kept), custom_call_target="tpu_custom_call" | custom-call | tf_op jit(solution)/shard_map/pallas_call | solution.py:156
  24.5 0.1 collective-permute-start.2
  24.5 1.1 %collective-permute-done.2.received = f32[1,512]{1,0:T(1,128)S(1)} collective-permute-done((f32[1,512]{1,0:T(1,128)S(1)}, f32[1,512]{1,0:T(1,128)S(1)}, u32[]{:S(2)}, u32[]{:S(2)}) %collective-permute-start.2) | collective-permute-done | bytes 2080 | tf_op jit(solution)/shard_map/ppermute | solution.py:34
  25.7 0.2 collective-permute-start.3
  25.9 1.0 %collective-permute-done.3.received = f32[1,512]{1,0:T(1,128)S(1)} collective-permute-done((f32[1,512]{1,0:T(1,128)S(1)}, f32[1,512]{1,0:T(1,128)S(1)}, u32[]{:S(2)}, u32[]{:S(2)}) %collective-permute-start.3) | collective-permute-done | bytes 2080 | tf_op jit(solution)/shard_map/ppermute | solution.py:34
  26.9 0.2 collective-permute-start.4
  27.0 1.0 %collective-permute-done.4.received = f32[1,512]{1,0:T(1,128)S(1)} collective-permute-done((f32[1,512]{1,0:T(1,128)S(1)}, f32[1,512]{1,0:T(1,128)S(1)}, u32[]{:S(2)}, u32[]{:S(2)}) %collective-permute-start.4) | collective-permute-done | bytes 2080 | tf_op jit(solution)/shard_map/ppermute | solution.py:34
  28.0 0.2 collective-permute-start.5
  28.2 1.0 %collective-permute-done.5.received = f32[1,512]{1,0:T(1,128)S(1)} collective-permute-done((f32[1,512]{1,0:T(1,128)S(1)}, f32[1,512]{1,0:T(1,128)S(1)}, u32[]{:S(2)}, u32[]{:S(2)}) %collective-permute-start.5) | collective-permute-done | bytes 2080 | tf_op jit(solution)/shard_map/ppermute | solution.py:34
  29.2 0.2 collective-permute-start.6
  29.4 1.0 %collective-permute-done.6.received = f32[1,512]{1,0:T(1,128)S(1)} collective-permute-done((f32[1,512]{1,0:T(1,128)S(1)}, f32[1,512]{1,0:T(1,128)S(1)}, u32[]{:S(2)}, u32[]{:S(2)}) %collective-permute-start.6) | collective-permute-done | bytes 2080 | tf_op jit(solution)/shard_map/ppermute | solution.py:34
  30.4 7.2 %collective-permute-start.7 = (f32[1,512]{1,0:T(1,128)S(1)}, f32[1,512]{1,0:T(1,128)S(1)}, u32[]{:S(2)}, u32[]{:S(2)}) collective-permute-start(f32[1,512]{1,0:T(1,128)S(1)} %get-tuple-element.31), channel_id=1, source_target_pairs={{0,1},{1,0},{2,3},{3,2},{4,5},{5,4},{6,7},{7,6},{8,9},{9,8},{10,11... | collective-permute-start | bytes 6152 | tf_op jit(solution)/shard_map/ppermute | solution.py:34
  37.6 1.6 %collective-permute-done.7.received = f32[1,512]{1,0:T(1,128)S(1)} collective-permute-done((f32[1,512]{1,0:T(1,128)S(1)}, f32[1,512]{1,0:T(1,128)S(1)}, u32[]{:S(2)}, u32[]{:S(2)}) %collective-permute-start.7) | collective-permute-done | bytes 2080 | tf_op jit(solution)/shard_map/ppermute | solution.py:34
  39.1 0.2 shard_map.43
  39.3 0.1 collective-permute-start.8
  39.4 3.6 %collective-permute-done.8.received = f32[1,512]{1,0:T(1,128)S(1)} collective-permute-done((f32[1,512]{1,0:T(1,128)S(1)}, f32[1,512]{1,0:T(1,128)S(1)}, u32[]{:S(2)}, u32[]{:S(2)}) %collective-permute-start.8) | collective-permute-done | bytes 2080 | tf_op jit(solution)/shard_map/ppermute | solution.py:34
  43.0 2.5 %shard_map.44 = f32[12,128]{1,0:T(8,128)} custom-call(f32[12,512,512]{2,1,0:T(8,128)S(1)} %copy-done, f32[12,512]{1,0:T(8,128)S(1)} %copy-done.1, f32[1,512]{1,0:T(1,128)S(1)} %collective-permute-done.8.received, f32[1,512]{1,0:T(1,128)S(1)} %get-tuple-element.34.kept), custom_call_target="tpu_custom_call" | custom-call | tf_op jit(solution)/shard_map/pallas_call | solution.py:156
  (10 shorter events, 0.0 us)
Async XLA Ops:
  0.7 1.2 %collective-permute-start = (f32[1,512]{1,0:T(1,128)S(1)}, f32[1,512]{1,0:T(1,128)S(1)}, u32[]{:S(2)}, u32[]{:S(2)}) collective-permute-start(f32[1,512]{1,0:T(1,128)S(1)} %constant_dynamic-update-slice_fusion.1), channel_id=1, source_target_pairs={{0,1},{1,0},{2,3},{3,2},{4,5},{5,4},{6,7},{7,6},{8,9},{9,8},{10,11... | collective-permute-start | bytes 6152 | tf_op jit(solution)/shard_map/ppermute | solution.py:47
  2.5 3.6 %collective-permute-start.1 = (f32[1,512]{1,0:T(1,128)S(1)}, f32[1,512]{1,0:T(1,128)S(1)}, u32[]{:S(2)}, u32[]{:S(2)}) collective-permute-start(f32[1,512]{1,0:T(1,128)S(1)} %constant_dynamic-update-slice_fusion), channel_id=1, source_target_pairs={{0,2},{1,3},{2,0},{3,1},{4,6},{5,7},{6,4},{7,5},{8,10},{9,11},{10,... | collective-permute-start | bytes 6152 | tf_op jit(solution)/shard_map/ppermute | solution.py:47
  6.1 4.6 %copy-start = (f32[12,512,512]{2,1,0:T(8,128)S(1)}, f32[12,512,512]{2,1,0:T(8,128)}, u32[]{:S(2)}) copy-start(f32[12,512,512]{2,1,0:T(8,128)} %jac.15) | copy-start | bytes 37748740
  10.7 0.8 %copy-start.1 = (f32[12,512]{1,0:T(8,128)S(1)}, f32[12,512]{1,0:T(8,128)}, u32[]{:S(2)}) copy-start(f32[12,512]{1,0:T(8,128)} %inc.15) | copy-start | bytes 73732
  24.5 1.2 %collective-permute-start.2 = (f32[1,512]{1,0:T(1,128)S(1)}, f32[1,512]{1,0:T(1,128)S(1)}, u32[]{:S(2)}, u32[]{:S(2)}) collective-permute-start(f32[1,512]{1,0:T(1,128)S(1)} %get-tuple-element.22), channel_id=1, source_target_pairs={{0,4},{1,5},{2,6},{3,7},{4,0},{5,1},{6,2},{7,3},{8,9},{9,8},{10,11... | collective-permute-start | bytes 6152 | tf_op jit(solution)/shard_map/ppermute | solution.py:34
  25.7 1.2 %collective-permute-start.3 = (f32[1,512]{1,0:T(1,128)S(1)}, f32[1,512]{1,0:T(1,128)S(1)}, u32[]{:S(2)}, u32[]{:S(2)}) collective-permute-start(f32[1,512]{1,0:T(1,128)S(1)} %get-tuple-element.23), channel_id=1, source_target_pairs={{0,1},{1,0},{2,3},{3,2},{4,8},{5,9},{6,10},{7,11},{8,4},{9,5},{10,... | collective-permute-start | bytes 6152 | tf_op jit(solution)/shard_map/ppermute | solution.py:34
  26.9 1.2 %collective-permute-start.4 = (f32[1,512]{1,0:T(1,128)S(1)}, f32[1,512]{1,0:T(1,128)S(1)}, u32[]{:S(2)}, u32[]{:S(2)}) collective-permute-start(f32[1,512]{1,0:T(1,128)S(1)} %get-tuple-element.25), channel_id=1, source_target_pairs={{0,1},{1,0},{2,3},{3,2},{4,5},{5,4},{6,7},{7,6},{8,12},{9,13},{10,... | collective-permute-start | bytes 6152 | tf_op jit(solution)/shard_map/ppermute | solution.py:34
  28.0 1.2 %collective-permute-start.5 = (f32[1,512]{1,0:T(1,128)S(1)}, f32[1,512]{1,0:T(1,128)S(1)}, u32[]{:S(2)}, u32[]{:S(2)}) collective-permute-start(f32[1,512]{1,0:T(1,128)S(1)} %get-tuple-element.27), channel_id=1, source_target_pairs={{0,1},{1,0},{2,3},{3,2},{4,5},{5,4},{6,7},{7,6},{8,9},{9,8},{10,11... | collective-permute-start | bytes 6152 | tf_op jit(solution)/shard_map/ppermute | solution.py:34
  29.2 1.2 %collective-permute-start.6 = (f32[1,512]{1,0:T(1,128)S(1)}, f32[1,512]{1,0:T(1,128)S(1)}, u32[]{:S(2)}, u32[]{:S(2)}) collective-permute-start(f32[1,512]{1,0:T(1,128)S(1)} %get-tuple-element.29), channel_id=1, source_target_pairs={{0,1},{1,0},{2,3},{3,2},{4,5},{5,4},{6,7},{7,6},{8,9},{9,8},{10,11... | collective-permute-start | bytes 6152 | tf_op jit(solution)/shard_map/ppermute | solution.py:34
  30.4 8.8 %collective-permute-start.7 = (f32[1,512]{1,0:T(1,128)S(1)}, f32[1,512]{1,0:T(1,128)S(1)}, u32[]{:S(2)}, u32[]{:S(2)}) collective-permute-start(f32[1,512]{1,0:T(1,128)S(1)} %get-tuple-element.31), channel_id=1, source_target_pairs={{0,1},{1,0},{2,3},{3,2},{4,5},{5,4},{6,7},{7,6},{8,9},{9,8},{10,11... | collective-permute-start | bytes 6152 | tf_op jit(solution)/shard_map/ppermute | solution.py:34
  39.3 3.7 %collective-permute-start.8 = (f32[1,512]{1,0:T(1,128)S(1)}, f32[1,512]{1,0:T(1,128)S(1)}, u32[]{:S(2)}, u32[]{:S(2)}) collective-permute-start(f32[1,512]{1,0:T(1,128)S(1)} %get-tuple-element.33), channel_id=1, source_target_pairs={{0,1},{1,0},{2,3},{3,2},{4,5},{5,4},{6,7},{7,6},{8,9},{9,8},{10,11... | collective-permute-start | bytes 6152 | tf_op jit(solution)/shard_map/ppermute | solution.py:34

commit v2 on v1

v2 whole, which is shorter than its diff:
```python
import functools

import jax
import jax.numpy as jnp
from jax import lax
from jax.experimental import pallas as pl
from jax.experimental.pallas import tpu as pltpu
from jax.sharding import PartitionSpec as P

AXES = ("tm", "col")
LANES = 128
VMEM = pl.BlockSpec(memory_space=pltpu.VMEM)
FAR = pl.BlockSpec(memory_space=pltpu.HBM)


def factors(segment, steps):
    wanted = 3 * segment + 1
    if isinstance(segment, int):
        return min(steps - 1, wanted)
    return jnp.minimum(steps - 1, wanted)


def swap_routes(size, moved):
    target = dict(moved)
    for device in range(size):
        partner = device ^ 1
        if device not in target and partner < size and partner not in target:
            target[device] = partner
            target[partner] = device
    return sorted(target.items())


def hop(block, segment, twist=0, rejoin=0):
    segments, parts = lax.axis_size("tm"), lax.axis_size("col")
    moved = {}
    for part in range(parts):
        here = segment * parts + part
        there = (segment + 1) * parts + (part ^ twist)
        moved[here] = there
        moved[there] = here
        if rejoin:
            moved[part] = part ^ rejoin
    return lax.ppermute(block, AXES, swap_routes(segments * parts, moved))


def swap_parts(block):
    parts = lax.axis_size("col")
    return lax.ppermute(block, "col", [(i, i ^ 1) for i in range(parts)])


def reduce_rows(total):
    diagonal = lax.broadcasted_iota(jnp.int32, (LANES, LANES), 0) == lax.broadcasted_iota(
        jnp.int32, (LANES, LANES), 1
    )
    column = jnp.sum(total, axis=1, keepdims=True)
    return jnp.sum(jnp.where(diagonal, column, 0.0), axis=0, keepdims=True)


def apply_block(rows_of, vector):
    total = None
    for left in range(0, vector.shape[1], LANES):
        term = rows_of(left) * vector[:, left : left + LANES]
        total = term if total is None else total + term
    return reduce_rows(total)


def apply_map(block_of, offset, vector):
    pieces = [
        apply_block(functools.partial(block_of, top), vector)
        for top in range(0, vector.shape[1], LANES)
    ]
    return jnp.concatenate(pieces, axis=1) + offset


def apply_whole(whole, offset, vector):
    return apply_map(
        lambda top, left: whole[pl.ds(top, LANES), pl.ds(left, LANES)], offset, vector
    )


def step(jac, inc, t, vector):
    return apply_map(
        lambda top, left: jac[t, pl.ds(top, LANES), pl.ds(left, LANES)],
        inc[pl.ds(t, 1), :],
        vector,
    )


def run_steps(jac, inc, first, last, vector):
    return lax.fori_loop(first, last, lambda t, v: step(jac, inc, t, v), vector)


def own_part(vector, part):
    index = lax.axis_index("col")
    own = vector[:, 0:part]
    for other in range(1, vector.shape[1] // part):
        own = jnp.where(index == other, vector[:, other * part : (other + 1) * part], own)
    return own


def halves(value):
    high = value.astype(jnp.bfloat16)
    return high, (value - high.astype(jnp.float32)).astype(jnp.bfloat16)


def product(left, right):
    left_high, left_low = halves(left)
    right_high, right_low = halves(right)

    def dot(a, b):
        return jnp.dot(a, b, preferred_element_type=jnp.float32)

    return dot(left_high, right_high) + (dot(left_high, right_low) + dot(left_low, right_high))


def first_kernel(jac_far, inc_far, own_far, jac, inc, sent, whole, offset, rows, offs, own, sems):
    steps, order, _ = jac.shape
    width = own.shape[1]
    segment = lax.axis_index("tm")
    index = lax.axis_index("col")

    def jac_copy(t):
        return pltpu.make_async_copy(jac_far.at[t], jac.at[t], sems.at[t])

    small = [
        pltpu.make_async_copy(own_far, own, sems.at[steps]),
        pltpu.make_async_copy(inc_far, inc, sems.at[steps + 1]),
    ]
    for copy in small:
        copy.start()
    for t in range(steps):
        jac_copy(t).start()
    for copy in small:
        copy.wait()

    @pl.when(segment == 0)
    def _():
        block = own[...]
        zero = jnp.zeros_like(block)
        vector = jnp.concatenate(
            [jnp.where(index == place, block, zero) for place in range(order // width)], axis=1
        )
        sent[:, order:] = vector

        def body(t, current):
            jac_copy(t).wait()
            added = inc[pl.ds(t, 1), :]
            return apply_map(
                lambda top, left: jac[t, pl.ds(top, LANES), pl.ds(left, LANES)],
                jnp.where(index == 0, added, jnp.zeros_like(added)),
                current,
            )

        sent[:, :order] = lax.fori_loop(0, steps, body, vector)

    @pl.when(segment > 0)
    def _():
        own_rows = pl.ds(pl.multiple_of(index * width, width), width)
        jac_copy(0).wait()
        whole[...] = jac[0]
        rows[0] = jac[0, own_rows, :]
        first = inc[0:1, :]
        offs[0:1, :] = own_part(first, width)
        count = factors(segment, steps)

        def body(t, carry):
            jac_copy(t).wait()
            whole[...] = product(jac[t], whole[...])
            carry = step(jac, inc, t, carry)
            rows[t] = whole[own_rows, :]
            offs[pl.ds(t, 1), :] = own_part(carry, width)
            return carry

        offset[...] = lax.fori_loop(1, 1 + count, body, first)

        def finish(t, carry):
            jac_copy(t).wait()
            return carry

        lax.fori_loop(1 + count, steps, finish, 0)


def join_kernel(mine, theirs, out, kept):
    order = out.shape[1]
    total = mine[...] + theirs[...]
    out[...] = total[:, :order]
    kept[...] = total[:, order:]


def hop_kernel(k, rejoin, jac, inc, whole, offset, kept, *refs):
    received, (out, start) = refs[:-2], refs[-2:]
    here = lax.axis_index("tm") == k
    steps = jac.shape[0]

    @pl.when(here)
    def _():
        vector = received[0][...]
        for other in received[1:]:
            vector = vector + other[...]
        start[...] = vector
        done = 1 + factors(k, steps)
        vector = apply_whole(whole, offset[...], vector)
        out[...] = run_steps(jac, inc, done, steps, vector) if done < steps else vector

    @pl.when(jnp.logical_not(here))
    def _():
        vector = kept[...]
        if rejoin:
            vector = jnp.where(lax.axis_index("tm") == 0, vector + received[0][...], vector)
        start[...] = vector
        out[...] = vector


def write_states(segment, jac, inc, rows, offs, vector, out):
    steps, part = out.shape
    prepared = jnp.logical_and(segment > 0, factors(segment, steps) == steps - 1)

    @pl.when(prepared)
    def _():
        for t in range(steps):
            own = apply_block(lambda left, t=t: rows[t, :, pl.ds(left, LANES)], vector)
            out[pl.ds(t, 1), :] = own + offs[pl.ds(t, 1), :]

    @pl.when(jnp.logical_not(prepared))
    def _():
        def body(t, v):
            v = step(jac, inc, t, v)
            out[pl.ds(t, 1), :] = own_part(v, part)
            return v

        lax.fori_loop(0, steps, body, vector)


def states_kernel(last, jac, inc, rows, offs, kept, out):
    segment = lax.axis_index("tm")

    @pl.when(segment != last)
    def _():
        write_states(segment, jac, inc, rows, offs, kept[...], out)


def last_kernel(last, jac, inc, rows, offs, received, before, out, scratch, sem):
    del before
    segment = lax.axis_index("tm")

    @pl.when(segment == last)
    def _():
        write_states(segment, jac, inc, rows, offs, received[...], scratch)
        copy = pltpu.make_async_copy(scratch, out, sem)
        copy.start()
        copy.wait()


def call(kernel, outs, *args, limit=4 << 20, far=(), far_out=False, scratch=(), aliases=None, work=0):
    return pl.pallas_call(
        kernel,
        out_shape=outs,
        in_specs=[FAR if place in far else VMEM for place in range(len(args))],
        out_specs=jax.tree.map(lambda _: FAR if far_out else VMEM, outs),
        scratch_shapes=scratch,
        input_output_aliases=aliases or {},
        cost_estimate=pl.CostEstimate(flops=work, bytes_accessed=work, transcendentals=0),
        compiler_params=pltpu.CompilerParams(vmem_limit_bytes=limit),
    )(*args)


def body(jacobians, increments, initial):
    segments, parts = lax.axis_size("tm"), lax.axis_size("col")
    steps, order, _ = jacobians.shape
    width = initial.shape[0]
    f32 = jnp.float32
    row = pltpu.VMEM((1, order), f32)
    far = [
        pltpu.with_memory_space_constraint(array, pltpu.HBM)
        for array in (jacobians, increments, initial[None, :])
    ]
    jac, inc, sent, whole, offset, rows, offs = call(
        first_kernel,
        (
            pltpu.VMEM(jacobians.shape, f32),
            pltpu.VMEM(increments.shape, f32),
            pltpu.VMEM((1, 2 * order), f32),
            pltpu.VMEM((order, order), f32),
            row,
            pltpu.VMEM((steps, width, order), f32),
            pltpu.VMEM((steps, width), f32),
        ),
        *far,
        far=(0, 1, 2),
        limit=16 << 20,
        scratch=[pltpu.VMEM((1, width), f32), pltpu.SemaphoreType.DMA((steps + 2,))],
    )
    out, kept = call(join_kernel, (row, row), sent, swap_parts(sent))
    last = segments - 1
    for k in range(1, segments):
        if k == 1:
            received = [hop(out, 0, twist) for twist in range(0, parts, 2)]
        elif k == 3:
            received = [hop(out, 2, rejoin=2)]
        else:
            received = [hop(out, k - 1)]
        if k < last:
            out, kept = call(
                functools.partial(hop_kernel, k, k == 3),
                (row, row),
                jac,
                inc,
                whole,
                offset,
                kept,
                *received,
            )
    shape = jax.ShapeDtypeStruct((steps, width), f32)
    before = call(
        functools.partial(states_kernel, last),
        shape,
        jac,
        inc,
        rows,
        offs,
        kept,
        work=steps * order * order * 4,
    )
    return call(
        functools.partial(last_kernel, last),
        shape,
        jac,
        inc,
        rows,
        offs,
        received[0],
        before,
        far=(5,),
        far_out=True,
        scratch=[pltpu.VMEM((steps, width), f32), pltpu.SemaphoreType.DMA],
        aliases={5: 0},
    )


def solution(mesh):
    return jax.shard_map(
        body,
        mesh=mesh,
        in_specs=(P("tm", None, None), P("tm", None), P("col")),
        out_specs=P("tm", "col"),
        check_vma=False,
    )
```

time: 45.7 us -> 32.2 us (0.70)
  local copies, waits for them, and re-layouts: 6 us -> 0 us
  waiting for transfers between devices: 13.5 us -> 9.47 us
  Pallas kernels: 15.7 us -> 14.2 us
  starting transfers between devices: 9.56 us -> 8.34 us
  other arithmetic: 0.67 us -> 0 us
    unnamed x4 -> x0, local copies, waits for them, and re-layouts: 5.33 us -> none
    ppermute x9, waiting for transfers between devices: 13.5 us -> 9.47 us  [the longest x8 8.32 us: hop(): return lax.ppermute(block, AXES, swap_routes(segments * parts, moved))]
    pallas_call x8 -> x10, Pallas kernels: 15.7 us -> 14.2 us  [call(): pl.pallas_call(kernel, out_shape=outs, in_specs=[FAR if place in far else...]
    ppermute x9, starting transfers between devices: 9.56 us -> 8.34 us  [the longest x8 8.27 us: hop(): return lax.ppermute(block, AXES, swap_routes(segments * parts, moved))]
    add x2 -> x0, other arithmetic: 0.67 us -> none  [gather_parts(): full = full + lax.ppermute(full, 'col', route)]
    dynamic_update_slice x1 -> x0, local copies, waits for them, and re-layouts: 0.66 us -> none  [gather_parts(): lax.dynamic_update_slice(jnp.zeros((1, width * parts), own.dtype), own, (...]
  transfers between devices with their start and end apart: 9 -> 9, of which waited for: 9 -> 9; matrix products, arithmetic and copies ran while one was open for 0% -> 0% of each run, Pallas kernels for 0% -> 3%
where the time goes in v2:
time: 32.2 us; the launch traced here: 32.1 us
  Pallas kernels  14.2 us (44%)
  waiting for transfers between devices  9.47 us (29%)
  starting transfers between devices  8.34 us (26%)
    pallas_call x10, Pallas kernels, call(): pl.pallas_call(kernel, out_shape=outs, in_specs=[FAR if place in far else...  14.2 us
    ppermute x8, waiting for transfers between devices, hop(): return lax.ppermute(block, AXES, swap_routes(segments * parts, moved))  8.32 us
    ppermute x8, starting transfers between devices, hop(): return lax.ppermute(block, AXES, swap_routes(segments * parts, moved))  8.27 us
    ppermute x1, waiting for transfers between devices, swap_parts(): return lax.ppermute(block, 'col', [(i, i ^ 1) for i in range(parts)])  1.15 us
  transfers between devices with their start and end apart: 9, of which 9 were waited for; matrix products, arithmetic and copies ran while one was open for 0% of the time, Pallas kernels for 3%

profile of v2, /device:TPU:24, one launch (start us, length us, event | category | flops | bytes accessed | tf_op | source)
XLA Modules:
  0.0 32.1 jit_solution(14890125394965921036)
XLA Ops:
  0.0 13.1 %shard_map.37 = (f32[12,512,512]{2,1,0:T(8,128)S(1)}, f32[12,512]{1,0:T(8,128)S(1)}, f32[1,1024]{1,0:T(1,128)S(1)}, f32[512,512]{1,0:T(8,128)S(1)}, f32[1,512]{1...) custom-call(f32[12,512,512]{2,1,0:T(8,128)} %jac_far.1, f32[12,512]{1,0:T(8,128)} %inc_far.1, ...), custom_call_target="tpu_custom_call" | custom-call | tf_op jit(solution)/shard_map/pallas_call | solution.py:255
  13.1 0.1 collective-permute-start
  13.2 1.2 %collective-permute-done.theirs = f32[1,1024]{1,0:T(1,128)S(1)} collective-permute-done((f32[1,1024]{1,0:T(1,128)S(1)}, f32[1,1024]{1,0:T(1,128)S(1)}, u32[]{:S(2)}, u32[]{:S(2)}) %collective-permute-start) | collective-permute-done | bytes 4128 | tf_op jit(solution)/shard_map/ppermute | solution.py:48
  14.4 0.2 collective-permute-start.2
  14.5 0.3 %collective-permute-start.1 = (f32[1,512]{1,0:T(1,128)S(1)}, f32[1,512]{1,0:T(1,128)S(1)}, u32[]{:S(2)}, u32[]{:S(2)}) collective-permute-start(f32[1,512]{1,0:T(1,128)S(1)} %get-tuple-element.34), channel_id=1, source_target_pairs={{0,4},{1,5},{2,6},{3,7},{4,0},{5,1},{6,2},{7,3},{8,9},{9,8},{10,11... | collective-permute-start | bytes 6152 | tf_op jit(solution)/shard_map/ppermute | solution.py:43
  14.9 0.7 %collective-permute-done.2.refs_1_ = f32[1,512]{1,0:T(1,128)S(1)} collective-permute-done((f32[1,512]{1,0:T(1,128)S(1)}, f32[1,512]{1,0:T(1,128)S(1)}, u32[]{:S(2)}, u32[]{:S(2)}) %collective-permute-start.2) | collective-permute-done | bytes 2080 | tf_op jit(solution)/shard_map/ppermute | solution.py:43
  15.5 0.2 collective-permute-done.1.refs_0_
  15.7 0.3 %collective-permute-start.3 = (f32[1,512]{1,0:T(1,128)S(1)}, f32[1,512]{1,0:T(1,128)S(1)}, u32[]{:S(2)}, u32[]{:S(2)}) collective-permute-start(f32[1,512]{1,0:T(1,128)S(1)} %get-tuple-element.36), channel_id=1, source_target_pairs={{0,1},{1,0},{2,3},{3,2},{4,8},{5,9},{6,10},{7,11},{8,4},{9,5},{10,... | collective-permute-start | bytes 6152 | tf_op jit(solution)/shard_map/ppermute | solution.py:43
  16.1 0.8 %collective-permute-done.3.refs_0_ = f32[1,512]{1,0:T(1,128)S(1)} collective-permute-done((f32[1,512]{1,0:T(1,128)S(1)}, f32[1,512]{1,0:T(1,128)S(1)}, u32[]{:S(2)}, u32[]{:S(2)}) %collective-permute-start.3) | collective-permute-done | bytes 2080 | tf_op jit(solution)/shard_map/ppermute | solution.py:43
  16.9 0.3 %collective-permute-start.4 = (f32[1,512]{1,0:T(1,128)S(1)}, f32[1,512]{1,0:T(1,128)S(1)}, u32[]{:S(2)}, u32[]{:S(2)}) collective-permute-start(f32[1,512]{1,0:T(1,128)S(1)} %get-tuple-element.38), channel_id=1, source_target_pairs={{0,2},{1,3},{2,0},{3,1},{4,5},{5,4},{6,7},{7,6},{8,12},{9,13},{10,... | collective-permute-start | bytes 6152 | tf_op jit(solution)/shard_map/ppermute | solution.py:43
  17.2 0.8 %collective-permute-done.4.refs_0_ = f32[1,512]{1,0:T(1,128)S(1)} collective-permute-done((f32[1,512]{1,0:T(1,128)S(1)}, f32[1,512]{1,0:T(1,128)S(1)}, u32[]{:S(2)}, u32[]{:S(2)}) %collective-permute-start.4) | collective-permute-done | bytes 2080 | tf_op jit(solution)/shard_map/ppermute | solution.py:43
  18.0 0.3 %collective-permute-start.5 = (f32[1,512]{1,0:T(1,128)S(1)}, f32[1,512]{1,0:T(1,128)S(1)}, u32[]{:S(2)}, u32[]{:S(2)}) collective-permute-start(f32[1,512]{1,0:T(1,128)S(1)} %get-tuple-element.40), channel_id=1, source_target_pairs={{0,1},{1,0},{2,3},{3,2},{4,5},{5,4},{6,7},{7,6},{8,9},{9,8},{10,11... | collective-permute-start | bytes 6152 | tf_op jit(solution)/shard_map/ppermute | solution.py:43
  18.4 0.8 %collective-permute-done.5.refs_0_ = f32[1,512]{1,0:T(1,128)S(1)} collective-permute-done((f32[1,512]{1,0:T(1,128)S(1)}, f32[1,512]{1,0:T(1,128)S(1)}, u32[]{:S(2)}, u32[]{:S(2)}) %collective-permute-start.5) | collective-permute-done | bytes 2080 | tf_op jit(solution)/shard_map/ppermute | solution.py:43
  19.2 0.3 %collective-permute-start.6 = (f32[1,512]{1,0:T(1,128)S(1)}, f32[1,512]{1,0:T(1,128)S(1)}, u32[]{:S(2)}, u32[]{:S(2)}) collective-permute-start(f32[1,512]{1,0:T(1,128)S(1)} %get-tuple-element.42), channel_id=1, source_target_pairs={{0,1},{1,0},{2,3},{3,2},{4,5},{5,4},{6,7},{7,6},{8,9},{9,8},{10,11... | collective-permute-start | bytes 6152 | tf_op jit(solution)/shard_map/ppermute | solution.py:43
  19.6 0.8 %collective-permute-done.6.refs_0_ = f32[1,512]{1,0:T(1,128)S(1)} collective-permute-done((f32[1,512]{1,0:T(1,128)S(1)}, f32[1,512]{1,0:T(1,128)S(1)}, u32[]{:S(2)}, u32[]{:S(2)}) %collective-permute-start.6) | collective-permute-done | bytes 2080 | tf_op jit(solution)/shard_map/ppermute | solution.py:43
  20.4 6.3 %collective-permute-start.7 = (f32[1,512]{1,0:T(1,128)S(1)}, f32[1,512]{1,0:T(1,128)S(1)}, u32[]{:S(2)}, u32[]{:S(2)}) collective-permute-start(f32[1,512]{1,0:T(1,128)S(1)} %get-tuple-element.44), channel_id=1, source_target_pairs={{0,1},{1,0},{2,3},{3,2},{4,5},{5,4},{6,7},{7,6},{8,9},{9,8},{10,11... | collective-permute-start | bytes 6152 | tf_op jit(solution)/shard_map/ppermute | solution.py:43
  26.7 1.6 %collective-permute-done.7.refs_0_ = f32[1,512]{1,0:T(1,128)S(1)} collective-permute-done((f32[1,512]{1,0:T(1,128)S(1)}, f32[1,512]{1,0:T(1,128)S(1)}, u32[]{:S(2)}, u32[]{:S(2)}) %collective-permute-start.7) | collective-permute-done | bytes 2080 | tf_op jit(solution)/shard_map/ppermute | solution.py:43
  28.3 0.2 shard_map.44
  28.4 0.1 collective-permute-start.8
  28.5 0.9 %shard_map.45.before = f32[12,128]{1,0:T(8,128)} custom-call(f32[12,512,512]{2,1,0:T(8,128)S(1)} %get-tuple-element.26.jac, f32[12,512]{1,0:T(8,128)S(1)} %get-tuple-element.27.inc, f32[12,128,512]{2,1,0:T(8,128)S(1)} %get-tuple-element.28.rows, f32[12,128]{1,0:T(8,128)S(1)} %get-tuple-element.29.offs, f32[1,512]{1,0:T(1,128)S(1)} %get-tuple-element.46.kept), custom_call_target="tpu_custom_call" | custom-call | flops 12582912 | bytes 12582912 | tf_op jit(solution)/shard_map/pallas_call | solution.py:255
  29.4 2.6 %collective-permute-done.8.received = f32[1,512]{1,0:T(1,128)S(1)} collective-permute-done((f32[1,512]{1,0:T(1,128)S(1)}, f32[1,512]{1,0:T(1,128)S(1)}, u32[]{:S(2)}, u32[]{:S(2)}) %collective-permute-start.8) | collective-permute-done | bytes 2080 | tf_op jit(solution)/shard_map/ppermute | solution.py:43
  (7 shorter events, 0.0 us)
Async XLA Ops:
  13.1 1.2 %collective-permute-start = (f32[1,1024]{1,0:T(1,128)S(1)}, f32[1,1024]{1,0:T(1,128)S(1)}, u32[]{:S(2)}, u32[]{:S(2)}) collective-permute-start(f32[1,1024]{1,0:T(1,128)S(1)} %get-tuple-element.32.mine), channel_id=1, source_target_pairs={{0,1},{1,0},{2,3},{3,2},{4,5},{5,4},{6,7},{7,6},{8,9},{9,8},{10,11... | collective-permute-start | bytes 12296 | tf_op jit(solution)/shard_map/ppermute | solution.py:48
  14.4 1.2 %collective-permute-start.2 = (f32[1,512]{1,0:T(1,128)S(1)}, f32[1,512]{1,0:T(1,128)S(1)}, u32[]{:S(2)}, u32[]{:S(2)}) collective-permute-start(f32[1,512]{1,0:T(1,128)S(1)} %get-tuple-element.34), channel_id=1, source_target_pairs={{0,6},{1,7},{2,4},{3,5},{4,2},{5,3},{6,0},{7,1},{8,9},{9,8},{10,11... | collective-permute-start | bytes 6152 | tf_op jit(solution)/shard_map/ppermute | solution.py:43
  14.5 1.2 %collective-permute-start.1 = (f32[1,512]{1,0:T(1,128)S(1)}, f32[1,512]{1,0:T(1,128)S(1)}, u32[]{:S(2)}, u32[]{:S(2)}) collective-permute-start(f32[1,512]{1,0:T(1,128)S(1)} %get-tuple-element.34), channel_id=1, source_target_pairs={{0,4},{1,5},{2,6},{3,7},{4,0},{5,1},{6,2},{7,3},{8,9},{9,8},{10,11... | collective-permute-start | bytes 6152 | tf_op jit(solution)/shard_map/ppermute | solution.py:43
  15.7 1.2 %collective-permute-start.3 = (f32[1,512]{1,0:T(1,128)S(1)}, f32[1,512]{1,0:T(1,128)S(1)}, u32[]{:S(2)}, u32[]{:S(2)}) collective-permute-start(f32[1,512]{1,0:T(1,128)S(1)} %get-tuple-element.36), channel_id=1, source_target_pairs={{0,1},{1,0},{2,3},{3,2},{4,8},{5,9},{6,10},{7,11},{8,4},{9,5},{10,... | collective-permute-start | bytes 6152 | tf_op jit(solution)/shard_map/ppermute | solution.py:43
  16.9 1.2 %collective-permute-start.4 = (f32[1,512]{1,0:T(1,128)S(1)}, f32[1,512]{1,0:T(1,128)S(1)}, u32[]{:S(2)}, u32[]{:S(2)}) collective-permute-start(f32[1,512]{1,0:T(1,128)S(1)} %get-tuple-element.38), channel_id=1, source_target_pairs={{0,2},{1,3},{2,0},{3,1},{4,5},{5,4},{6,7},{7,6},{8,12},{9,13},{10,... | collective-permute-start | bytes 6152 | tf_op jit(solution)/shard_map/ppermute | solution.py:43
  18.0 1.2 %collective-permute-start.5 = (f32[1,512]{1,0:T(1,128)S(1)}, f32[1,512]{1,0:T(1,128)S(1)}, u32[]{:S(2)}, u32[]{:S(2)}) collective-permute-start(f32[1,512]{1,0:T(1,128)S(1)} %get-tuple-element.40), channel_id=1, source_target_pairs={{0,1},{1,0},{2,3},{3,2},{4,5},{5,4},{6,7},{7,6},{8,9},{9,8},{10,11... | collective-permute-start | bytes 6152 | tf_op jit(solution)/shard_map/ppermute | solution.py:43
  19.2 1.2 %collective-permute-start.6 = (f32[1,512]{1,0:T(1,128)S(1)}, f32[1,512]{1,0:T(1,128)S(1)}, u32[]{:S(2)}, u32[]{:S(2)}) collective-permute-start(f32[1,512]{1,0:T(1,128)S(1)} %get-tuple-element.42), channel_id=1, source_target_pairs={{0,1},{1,0},{2,3},{3,2},{4,5},{5,4},{6,7},{7,6},{8,9},{9,8},{10,11... | collective-permute-start | bytes 6152 | tf_op jit(solution)/shard_map/ppermute | solution.py:43
  20.4 7.9 %collective-permute-start.7 = (f32[1,512]{1,0:T(1,128)S(1)}, f32[1,512]{1,0:T(1,128)S(1)}, u32[]{:S(2)}, u32[]{:S(2)}) collective-permute-start(f32[1,512]{1,0:T(1,128)S(1)} %get-tuple-element.44), channel_id=1, source_target_pairs={{0,1},{1,0},{2,3},{3,2},{4,5},{5,4},{6,7},{7,6},{8,9},{9,8},{10,11... | collective-permute-start | bytes 6152 | tf_op jit(solution)/shard_map/ppermute | solution.py:43
  28.4 3.7 %collective-permute-start.8 = (f32[1,512]{1,0:T(1,128)S(1)}, f32[1,512]{1,0:T(1,128)S(1)}, u32[]{:S(2)}, u32[]{:S(2)}) collective-permute-start(f32[1,512]{1,0:T(1,128)S(1)} %get-tuple-element.45), channel_id=1, source_target_pairs={{0,1},{1,0},{2,3},{3,2},{4,5},{5,4},{6,7},{7,6},{8,9},{9,8},{10,11... | collective-permute-start | bytes 6152 | tf_op jit(solution)/shard_map/ppermute | solution.py:43

commit v3 on v2

--- a/solution.py
+++ b/solution.py
@@ -9,15 +9,27 @@
 
 AXES = ("tm", "col")
 LANES = 128
+MERGE = 3
+JOINS = {2: (0,), 4: (1, 2, 3)}
+VIAS = (-1, 0)
+AHEAD = 7
+STAGES = (6, 8, 10)
 VMEM = pl.BlockSpec(memory_space=pltpu.VMEM)
 FAR = pl.BlockSpec(memory_space=pltpu.HBM)
 
 
+def smaller(a, b):
+    return min(a, b) if isinstance(a, int) and isinstance(b, int) else jnp.minimum(a, b)
+
+
+def first_factors(segment, steps):
+    wanted = 3 * segment - 3 + (segment == 1)
+    return smaller(smaller(wanted, AHEAD), steps - 1)
+
+
 def factors(segment, steps):
-    wanted = 3 * segment + 1
-    if isinstance(segment, int):
-        return min(steps - 1, wanted)
-    return jnp.minimum(steps - 1, wanted)
+    windows = segment - (segment == 1)
+    return smaller(first_factors(segment, steps) + windows, steps - 1)
 
 
 def swap_routes(size, moved):
@@ -30,16 +42,20 @@
     return sorted(target.items())
 
 
-def hop(block, segment, twist=0, rejoin=0):
+def hop(block, segment, twist=0, via=None, joined=()):
     segments, parts = lax.axis_size("tm"), lax.axis_size("col")
     moved = {}
     for part in range(parts):
         here = segment * parts + part
         there = (segment + 1) * parts + (part ^ twist)
         moved[here] = there
-        moved[there] = here
-        if rejoin:
-            moved[part] = part ^ rejoin
+        if via is None:
+            moved[there] = here ^ 1 if segment + 2 == segments and parts % 2 == 0 else here
+        else:
+            moved[there] = via * parts + part
+            moved[via * parts + part] = here
+        for other in joined:
+            moved[other * parts + part] = other * parts + (part ^ 2)
     return lax.ppermute(block, AXES, swap_routes(segments * parts, moved))
 
 
@@ -78,16 +94,20 @@
     )
 
 
-def step(jac, inc, t, vector):
+def masked(keep, added):
+    return added if keep is None else jnp.where(keep, added, jnp.zeros_like(added))
+
+
+def step(jac, inc, t, vector, keep=None):
     return apply_map(
         lambda top, left: jac[t, pl.ds(top, LANES), pl.ds(left, LANES)],
-        inc[pl.ds(t, 1), :],
+        masked(keep, inc[pl.ds(t, 1), :]),
         vector,
     )
 
 
-def run_steps(jac, inc, first, last, vector):
-    return lax.fori_loop(first, last, lambda t, v: step(jac, inc, t, v), vector)
+def run_steps(jac, inc, first, last, vector, keep):
+    return lax.fori_loop(first, last, lambda t, v: step(jac, inc, t, v, keep), vector)
 
 
 def own_part(vector, part):
@@ -113,14 +133,58 @@
     return dot(left_high, right_high) + (dot(left_high, right_low) + dot(left_low, right_high))
 
 
+def jac_copy(jac_far, jac, sems, t):
+    return pltpu.make_async_copy(jac_far.at[t], jac.at[t], sems.at[t])
+
+
+def stage_bounds(steps):
+    return [0] + [min(stage, steps) for stage in STAGES] + [steps]
+
+
+def add_factor(t, jac, inc, whole, rows, offs, carry):
+    width = offs.shape[1]
+    own_rows = pl.ds(pl.multiple_of(lax.axis_index("col") * width, width), width)
+    whole[...] = product(jac[t], whole[...])
+    carry = step(jac, inc, t, carry)
+    rows[t] = whole[own_rows, :]
+    offs[pl.ds(t, 1), :] = own_part(carry, width)
+    return carry
+
+
+def factor_kernel(window, jac_far, jac_in, inc, whole_in, offset_in, rows_in, offs_in, *refs):
+    jac, whole, offset, rows, offs, sems = refs
+    del jac_in, whole_in, offset_in, rows_in, offs_in
+    steps = jac.shape[0]
+    segment = lax.axis_index("tm")
+    t = first_factors(segment, steps) + window + 1
+    bounds = stage_bounds(steps)
+    late = range(*bounds[window + 1 : window + 3]) if window < 2 else ()
+
+    @pl.when(segment == 1)
+    def _():
+        for place in late:
+            jac_copy(jac_far, jac, sems, place).start()
+
+    @pl.when(jnp.logical_and(segment > max(window, 1), t < steps))
+    def _():
+        offset[...] = add_factor(t, jac, inc, whole, rows, offs, offset[...])
+
+    @pl.when(segment == 1)
+    def _():
+        for place in late:
+            jac_copy(jac_far, jac, sems, place).wait()
+
+
 def first_kernel(jac_far, inc_far, own_far, jac, inc, sent, whole, offset, rows, offs, own, sems):
     steps, order, _ = jac.shape
     width = own.shape[1]
     segment = lax.axis_index("tm")
     index = lax.axis_index("col")
-
-    def jac_copy(t):
-        return pltpu.make_async_copy(jac_far.at[t], jac.at[t], sems.at[t])
+    soon = stage_bounds(steps)[1]
+    now = jnp.where(segment == 1, soon, steps)
+
+    def arrived(t):
+        jac_copy(jac_far, jac, sems, t).wait()
 
     small = [
         pltpu.make_async_copy(own_far, own, sems.at[steps]),
@@ -128,8 +192,14 @@
     ]
     for copy in small:
         copy.start()
-    for t in range(steps):
-        jac_copy(t).start()
+    for t in range(soon):
+        jac_copy(jac_far, jac, sems, t).start()
+
+    @pl.when(segment != 1)
+    def _():
+        for t in range(soon, steps):
+            jac_copy(jac_far, jac, sems, t).start()
+
     for copy in small:
         copy.wait()
 
@@ -143,41 +213,32 @@
         sent[:, order:] = vector
 
         def body(t, current):
-            jac_copy(t).wait()
-            added = inc[pl.ds(t, 1), :]
-            return apply_map(
-                lambda top, left: jac[t, pl.ds(top, LANES), pl.ds(left, LANES)],
-                jnp.where(index == 0, added, jnp.zeros_like(added)),
-                current,
-            )
+            arrived(t)
+            return step(jac, inc, t, current, index == 0)
 
         sent[:, :order] = lax.fori_loop(0, steps, body, vector)
 
     @pl.when(segment > 0)
     def _():
         own_rows = pl.ds(pl.multiple_of(index * width, width), width)
-        jac_copy(0).wait()
+        arrived(0)
         whole[...] = jac[0]
         rows[0] = jac[0, own_rows, :]
         first = inc[0:1, :]
         offs[0:1, :] = own_part(first, width)
-        count = factors(segment, steps)
+        count = first_factors(segment, steps)
 
         def body(t, carry):
-            jac_copy(t).wait()
-            whole[...] = product(jac[t], whole[...])
-            carry = step(jac, inc, t, carry)
-            rows[t] = whole[own_rows, :]
-            offs[pl.ds(t, 1), :] = own_part(carry, width)
+            arrived(t)
+            return add_factor(t, jac, inc, whole, rows, offs, carry)
+
+        offset[...] = lax.fori_loop(1, 1 + count, body, first)
+
+        def finish(t, carry):
+            arrived(t)
             return carry
 
-        offset[...] = lax.fori_loop(1, 1 + count, body, first)
-
-        def finish(t, carry):
-            jac_copy(t).wait()
-            return carry
-
-        lax.fori_loop(1 + count, steps, finish, 0)
+        lax.fori_loop(1 + count, now, finish, 0)
 
 
 def join_kernel(mine, theirs, out, kept):
@@ -187,26 +248,41 @@
     kept[...] = total[:, order:]
 
 
-def hop_kernel(k, rejoin, jac, inc, whole, offset, kept, *refs):
-    received, (out, start) = refs[:-2], refs[-2:]
+def hop_kernel(k, joined, far, inc, whole, offset, kept, *refs):
+    jac = refs[0]
+    if far:
+        jac_far, received, (out, start, jac, sems) = refs[1], refs[2:-4], refs[-4:]
+    else:
+        received, (out, start) = refs[1:-2], refs[-2:]
     here = lax.axis_index("tm") == k
     steps = jac.shape[0]
+    late = stage_bounds(steps)[3] if far else steps
 
     @pl.when(here)
     def _():
+        for t in range(late, steps):
+            jac_copy(jac_far, jac, sems, t).start()
         vector = received[0][...]
         for other in received[1:]:
             vector = vector + other[...]
         start[...] = vector
+        keep = lax.axis_index("col") < 2 if k <= MERGE else None
         done = 1 + factors(k, steps)
-        vector = apply_whole(whole, offset[...], vector)
-        out[...] = run_steps(jac, inc, done, steps, vector) if done < steps else vector
+        vector = apply_whole(whole, masked(keep, offset[...]), vector)
+        if done < late:
+            vector = run_steps(jac, inc, done, late, vector, keep)
+        for t in range(late, steps):
+            jac_copy(jac_far, jac, sems, t).wait()
+            vector = step(jac, inc, t, vector, keep)
+        out[...] = vector
 
     @pl.when(jnp.logical_not(here))
     def _():
         vector = kept[...]
-        if rejoin:
-            vector = jnp.where(lax.axis_index("tm") == 0, vector + received[0][...], vector)
+        if joined:
+            segment = lax.axis_index("tm")
+            joins = functools.reduce(jnp.logical_or, [segment == other for other in joined])
+            vector = jnp.where(joins, vector + received[0][...], vector)
         start[...] = vector
         out[...] = vector
 
@@ -290,26 +366,65 @@
         limit=16 << 20,
         scratch=[pltpu.VMEM((1, width), f32), pltpu.SemaphoreType.DMA((steps + 2,))],
     )
-    out, kept = call(join_kernel, (row, row), sent, swap_parts(sent))
+    near = [jac, inc, whole, offset, rows, offs]
+
+    def more(window):
+        if window > 1 and all(
+            first_factors(segment, steps) + window >= steps - 1
+            for segment in range(window + 1, segments)
+        ):
+            return near
+        jac, inc, *rest = near
+        made = [pltpu.VMEM(array.shape, f32) for array in (jac, *rest)]
+        jac, *rest = call(
+            functools.partial(factor_kernel, window),
+            made,
+            far[0],
+            jac,
+            inc,
+            *rest,
+            far=(0,),
+            limit=16 << 20,
+            scratch=[pltpu.SemaphoreType.DMA((steps,))],
+            aliases={1: 0, 3: 1, 4: 2, 5: 3, 6: 4},
+            work=1 << 28,
+        )
+        return [jac, inc, *rest]
+
+    theirs = swap_parts(sent)
+    near = more(0)
+    out, kept = call(join_kernel, (row, row), sent, theirs)
     last = segments - 1
     for k in range(1, segments):
-        if k == 1:
-            received = [hop(out, 0, twist) for twist in range(0, parts, 2)]
-        elif k == 3:
-            received = [hop(out, 2, rejoin=2)]
+        joined = JOINS.get(k - 1, ())
+        if k == MERGE + 1:
+            received = [
+                hop(out, MERGE, 2 * twist, VIAS[twist] % segments, joined)
+                for twist in range(parts // 2)
+            ]
         else:
-            received = [hop(out, k - 1)]
+            received = [hop(out, k - 1, joined=joined)]
+        near = more(k)
+        jac, inc, whole, offset, rows, offs = near
         if k < last:
-            out, kept = call(
-                functools.partial(hop_kernel, k, k == 3),
-                (row, row),
-                jac,
+            first = k == 1
+            out, kept, *moved = call(
+                functools.partial(hop_kernel, k, joined, first),
+                [row, row] + [pltpu.VMEM(jac.shape, f32)] * first,
                 inc,
                 whole,
                 offset,
                 kept,
+                jac,
+                *[far[0]] * first,
                 *received,
+                far=(5,) if first else (),
+                scratch=[pltpu.SemaphoreType.DMA((steps,))] * first,
+                aliases={4: 2} if first else None,
             )
+            if first:
+                (jac,) = moved
+                near = [jac, *near[1:]]
     shape = jax.ShapeDtypeStruct((steps, width), f32)
     before = call(
         functools.partial(states_kernel, last),

time: 32.2 us -> 30.5 us (0.947)
  the two profiles are of different devices: /device:TPU:24 before, /device:TPU:11 now
where the time goes in v3:
time: 30.5 us; the launch traced here: 30.3 us
  Pallas kernels  14.8 us (49%)
  waiting for transfers between devices  8.72 us (29%)
  starting transfers between devices  6.72 us (22%)
    pallas_call x14, Pallas kernels, call(): pl.pallas_call(kernel, out_shape=outs, in_specs=[FAR if place in far else...  14.8 us
    ppermute x8, waiting for transfers between devices, hop(): return lax.ppermute(block, AXES, swap_routes(segments * parts, moved))  8.72 us
    ppermute x8, starting transfers between devices, hop(): return lax.ppermute(block, AXES, swap_routes(segments * parts, moved))  5.95 us
    ppermute x1, starting transfers between devices, swap_parts(): return lax.ppermute(block, 'col', [(i, i ^ 1) for i in range(parts)])  0.77 us
  transfers between devices with their start and end apart: 9, of which 5 were waited for; matrix products, arithmetic and copies ran while one was open for 0% of the time, Pallas kernels for 20%

profile of v3, /device:TPU:11, one launch (start us, length us, event | category | flops | bytes accessed | tf_op | source)
XLA Modules:
  0.0 30.3 jit_solution(8675328644014645971)
XLA Ops:
  0.0 8.1 %shard_map.37 = (f32[12,512,512]{2,1,0:T(8,128)S(1)}, f32[12,512]{1,0:T(8,128)S(1)}, f32[1,1024]{1,0:T(1,128)S(1)}, f32[512,512]{1,0:T(8,128)S(1)}, f32[1,512]{1...) custom-call(f32[12,512,512]{2,1,0:T(8,128)} %jac_far.9, f32[12,512]{1,0:T(8,128)} %inc_far.1, ...), custom_call_target="tpu_custom_call" | custom-call | tf_op jit(solution)/shard_map/pallas_call | solution.py:331
  8.1 0.8 %collective-permute-start = (f32[1,1024]{1,0:T(1,128)S(1)}, f32[1,1024]{1,0:T(1,128)S(1)}, u32[]{:S(2)}, u32[]{:S(2)}) collective-permute-start(f32[1,1024]{1,0:T(1,128)S(1)} %get-tuple-element.60.mine), channel_id=1, source_target_pairs={{0,1},{1,0},{2,3},{3,2},{4,5},{5,4},{6,7},{7,6},{8,9},{9,8},{10,11... | collective-permute-start | bytes 12296 | tf_op jit(solution)/shard_map/ppermute | solution.py:64
  8.8 1.2 %shard_map.38 = (f32[12,512,512]{2,1,0:T(8,128)S(1)}, f32[512,512]{1,0:T(8,128)S(1)}, f32[1,512]{1,0:T(1,128)S(1)}, f32[12,128,512]{2,1,0:T(8,128)S(1)}, f32[12,128]{1,0:T(8,128)S(1)}) custom-call(f32[12,512,512]{2,1,0:T(8,128)} %jac_far.9, ...), custom_call_target="tpu_custom_call", output_to_operand_aliasing={{0}: (1, {}), {1}: (3, {}), {2}: (4, {}), {3}: (5, {}), {4}... | custom-call | flops 268435456 | bytes 268435456 | tf_op jit(solution)/shard_map/pallas_call | solution.py:331
  10.0 0.0 collective-permute-done.theirs
  10.0 0.1 collective-permute-start.1
  10.1 1.2 %shard_map.39 = (f32[12,512,512]{2,1,0:T(8,128)S(1)}, f32[512,512]{1,0:T(8,128)S(1)}, f32[1,512]{1,0:T(1,128)S(1)}, f32[12,128,512]{2,1,0:T(8,128)S(1)}, f32[12,128]{1,0:T(8,128)S(1)}) custom-call(f32[12,512,512]{2,1,0:T(8,128)} %jac_far.9, ...), custom_call_target="tpu_custom_call", output_to_operand_aliasing={{0}: (1, {}), {1}: (3, {}), {2}: (4, {}), {3}: (5, {}), {4}... | custom-call | flops 268435456 | bytes 268435456 | tf_op jit(solution)/shard_map/pallas_call | solution.py:331
  11.3 0.0 collective-permute-done.1.refs_2_
  11.3 0.1 shard_map.41
  11.4 0.5 %collective-permute-start.2 = (f32[1,512]{1,0:T(1,128)S(1)}, f32[1,512]{1,0:T(1,128)S(1)}, u32[]{:S(2)}, u32[]{:S(2)}) collective-permute-start(f32[1,512]{1,0:T(1,128)S(1)} %get-tuple-element.78), channel_id=1, source_target_pairs={{0,1},{1,0},{2,3},{3,2},{4,8},{5,9},{6,10},{7,11},{8,4},{9,5},{10,... | collective-permute-start | bytes 6152 | tf_op jit(solution)/shard_map/ppermute | solution.py:59
  12.0 1.2 %shard_map.42 = (f32[12,512,512]{2,1,0:T(8,128)S(1)}, f32[512,512]{1,0:T(8,128)S(1)}, f32[1,512]{1,0:T(1,128)S(1)}, f32[12,128,512]{2,1,0:T(8,128)S(1)}, f32[12,128]{1,0:T(8,128)S(1)}) custom-call(f32[12,512,512]{2,1,0:T(8,128)} %jac_far.9, ...), custom_call_target="tpu_custom_call", output_to_operand_aliasing={{0}: (1, {}), {1}: (3, {}), {2}: (4, {}), {3}: (5, {}), {4}... | custom-call | flops 268435456 | bytes 268435456 | tf_op jit(solution)/shard_map/pallas_call | solution.py:331
  13.1 0.0 collective-permute-done.2.refs_1_
  13.2 0.1 collective-permute-start.3
  13.3 0.1 shard_map.43
  13.4 2.3 %collective-permute-done.3.refs_1_ = f32[1,512]{1,0:T(1,128)S(1)} collective-permute-done((f32[1,512]{1,0:T(1,128)S(1)}, f32[1,512]{1,0:T(1,128)S(1)}, u32[]{:S(2)}, u32[]{:S(2)}) %collective-permute-start.3) | collective-permute-done | bytes 2080 | tf_op jit(solution)/shard_map/ppermute | solution.py:59
  15.7 0.5 %shard_map.45 = (f32[1,512]{1,0:T(1,128)S(1)}, f32[1,512]{1,0:T(1,128)S(1)}) custom-call(f32[12,512]{1,0:T(8,128)S(1)} %get-tuple-element.47.inc, f32[512,512]{1,0:T(8,128)S(1)} %get-tuple-element.75.whole, f32[1,512]{1,0:T(1,128)S(1)} %get-tuple-element.76.offset, f32[1,512]{1,0:T(1,128)S(1)} %get-tuple-element.79.kept, ...), custom_call_target="tpu_custom_call" | custom-call | tf_op jit(solution)/shard_map/pallas_call | solution.py:331
  16.2 1.7 %collective-permute-start.5 = (f32[1,512]{1,0:T(1,128)S(1)}, f32[1,512]{1,0:T(1,128)S(1)}, u32[]{:S(2)}, u32[]{:S(2)}) collective-permute-start(f32[1,512]{1,0:T(1,128)S(1)} %get-tuple-element.82), channel_id=1, source_target_pairs={{0,12},{1,13},{2,14},{3,15},{4,5},{5,4},{6,7},{7,6},{8,9},{9,8},{1... | collective-permute-start | bytes 6152 | tf_op jit(solution)/shard_map/ppermute | solution.py:59
  17.8 1.7 %collective-permute-done.5.refs_2_ = f32[1,512]{1,0:T(1,128)S(1)} collective-permute-done((f32[1,512]{1,0:T(1,128)S(1)}, f32[1,512]{1,0:T(1,128)S(1)}, u32[]{:S(2)}, u32[]{:S(2)}) %collective-permute-start.5) | collective-permute-done | bytes 2080 | tf_op jit(solution)/shard_map/ppermute | solution.py:59
  19.5 1.6 %collective-permute-done.4.refs_1_ = f32[1,512]{1,0:T(1,128)S(1)} collective-permute-done((f32[1,512]{1,0:T(1,128)S(1)}, f32[1,512]{1,0:T(1,128)S(1)}, u32[]{:S(2)}, u32[]{:S(2)}) %collective-permute-start.4) | collective-permute-done | bytes 2080 | tf_op jit(solution)/shard_map/ppermute | solution.py:59
  21.2 0.2 collective-permute-start.6
  21.3 2.3 %collective-permute-done.6.refs_1_ = f32[1,512]{1,0:T(1,128)S(1)} collective-permute-done((f32[1,512]{1,0:T(1,128)S(1)}, f32[1,512]{1,0:T(1,128)S(1)}, u32[]{:S(2)}, u32[]{:S(2)}) %collective-permute-start.6) | collective-permute-done | bytes 2080 | tf_op jit(solution)/shard_map/ppermute | solution.py:59
  23.6 3.0 %collective-permute-start.7 = (f32[1,512]{1,0:T(1,128)S(1)}, f32[1,512]{1,0:T(1,128)S(1)}, u32[]{:S(2)}, u32[]{:S(2)}) collective-permute-start(f32[1,512]{1,0:T(1,128)S(1)} %get-tuple-element.86), channel_id=1, source_target_pairs={{0,1},{1,0},{2,3},{3,2},{4,5},{5,4},{6,7},{7,6},{8,9},{9,8},{10,11... | collective-permute-start | bytes 6152 | tf_op jit(solution)/shard_map/ppermute | solution.py:59
  26.6 0.8 %collective-permute-done.7.refs_1_ = f32[1,512]{1,0:T(1,128)S(1)} collective-permute-done((f32[1,512]{1,0:T(1,128)S(1)}, f32[1,512]{1,0:T(1,128)S(1)}, u32[]{:S(2)}, u32[]{:S(2)}) %collective-permute-start.7) | collective-permute-done | bytes 2080 | tf_op jit(solution)/shard_map/ppermute | solution.py:59
  27.5 0.3 %collective-permute-start.8 = (f32[1,512]{1,0:T(1,128)S(1)}, f32[1,512]{1,0:T(1,128)S(1)}, u32[]{:S(2)}, u32[]{:S(2)}) collective-permute-start(f32[1,512]{1,0:T(1,128)S(1)} %get-tuple-element.87), channel_id=1, source_target_pairs={{0,1},{1,0},{2,3},{3,2},{4,5},{5,4},{6,7},{7,6},{8,9},{9,8},{10,11... | collective-permute-start | bytes 6152 | tf_op jit(solution)/shard_map/ppermute | solution.py:59
  27.8 2.5 %shard_map.49.before = f32[12,128]{1,0:T(8,128)} custom-call(f32[12,512,512]{2,1,0:T(8,128)S(1)} %get-tuple-element.72.refs_0_.jac, f32[12,512]{1,0:T(8,128)S(1)} %get-tuple-element.47.inc, f32[12,128,512]{2,1,0:T(8,128)S(1)} %get-tuple-element.73.rows, f32[12,128]{1,0:T(8,128)S(1)} %get-tuple-element.74.offs, f32[1,512]{1,0:T(1,128)S(1)} %get-tuple-element.88.kept), custom_call_target="tpu_custom_call" | custom-call | flops 12582912 | bytes 12582912 | tf_op jit(solution)/shard_map/pallas_call | solution.py:331
  (8 shorter events, 0.1 us)
Async XLA Ops:
  8.1 1.9 %collective-permute-start = (f32[1,1024]{1,0:T(1,128)S(1)}, f32[1,1024]{1,0:T(1,128)S(1)}, u32[]{:S(2)}, u32[]{:S(2)}) collective-permute-start(f32[1,1024]{1,0:T(1,128)S(1)} %get-tuple-element.60.mine), channel_id=1, source_target_pairs={{0,1},{1,0},{2,3},{3,2},{4,5},{5,4},{6,7},{7,6},{8,9},{9,8},{10,11... | collective-permute-start | bytes 12296 | tf_op jit(solution)/shard_map/ppermute | solution.py:64
  10.0 1.3 %collective-permute-start.1 = (f32[1,512]{1,0:T(1,128)S(1)}, f32[1,512]{1,0:T(1,128)S(1)}, u32[]{:S(2)}, u32[]{:S(2)}) collective-permute-start(f32[1,512]{1,0:T(1,128)S(1)} %get-tuple-element.63), channel_id=1, source_target_pairs={{0,4},{1,5},{2,6},{3,7},{4,0},{5,1},{6,2},{7,3},{8,9},{9,8},{10,11... | collective-permute-start | bytes 6152 | tf_op jit(solution)/shard_map/ppermute | solution.py:59
  11.4 1.7 %collective-permute-start.2 = (f32[1,512]{1,0:T(1,128)S(1)}, f32[1,512]{1,0:T(1,128)S(1)}, u32[]{:S(2)}, u32[]{:S(2)}) collective-permute-start(f32[1,512]{1,0:T(1,128)S(1)} %get-tuple-element.78), channel_id=1, source_target_pairs={{0,1},{1,0},{2,3},{3,2},{4,8},{5,9},{6,10},{7,11},{8,4},{9,5},{10,... | collective-permute-start | bytes 6152 | tf_op jit(solution)/shard_map/ppermute | solution.py:59
  13.2 2.5 %collective-permute-start.3 = (f32[1,512]{1,0:T(1,128)S(1)}, f32[1,512]{1,0:T(1,128)S(1)}, u32[]{:S(2)}, u32[]{:S(2)}) collective-permute-start(f32[1,512]{1,0:T(1,128)S(1)} %get-tuple-element.80), channel_id=1, source_target_pairs={{0,2},{1,3},{2,0},{3,1},{4,5},{5,4},{6,7},{7,6},{8,12},{9,13},{10,... | collective-permute-start | bytes 6152 | tf_op jit(solution)/shard_map/ppermute | solution.py:59
  16.2 3.4 %collective-permute-start.5 = (f32[1,512]{1,0:T(1,128)S(1)}, f32[1,512]{1,0:T(1,128)S(1)}, u32[]{:S(2)}, u32[]{:S(2)}) collective-permute-start(f32[1,512]{1,0:T(1,128)S(1)} %get-tuple-element.82), channel_id=1, source_target_pairs={{0,12},{1,13},{2,14},{3,15},{4,5},{5,4},{6,7},{7,6},{8,9},{9,8},{1... | collective-permute-start | bytes 6152 | tf_op jit(solution)/shard_map/ppermute | solution.py:59
  17.8 3.3 %collective-permute-start.4 = (f32[1,512]{1,0:T(1,128)S(1)}, f32[1,512]{1,0:T(1,128)S(1)}, u32[]{:S(2)}, u32[]{:S(2)}) collective-permute-start(f32[1,512]{1,0:T(1,128)S(1)} %get-tuple-element.82), channel_id=1, source_target_pairs={{0,1},{1,0},{2,3},{3,2},{4,5},{5,4},{6,7},{7,6},{8,9},{9,8},{10,11... | collective-permute-start | bytes 6152 | tf_op jit(solution)/shard_map/ppermute | solution.py:59
  21.2 2.4 %collective-permute-start.6 = (f32[1,512]{1,0:T(1,128)S(1)}, f32[1,512]{1,0:T(1,128)S(1)}, u32[]{:S(2)}, u32[]{:S(2)}) collective-permute-start(f32[1,512]{1,0:T(1,128)S(1)} %get-tuple-element.84), channel_id=1, source_target_pairs={{0,1},{1,0},{2,3},{3,2},{4,6},{5,7},{6,4},{7,5},{8,10},{9,11},{10,... | collective-permute-start | bytes 6152 | tf_op jit(solution)/shard_map/ppermute | solution.py:59
  23.6 3.9 %collective-permute-start.7 = (f32[1,512]{1,0:T(1,128)S(1)}, f32[1,512]{1,0:T(1,128)S(1)}, u32[]{:S(2)}, u32[]{:S(2)}) collective-permute-start(f32[1,512]{1,0:T(1,128)S(1)} %get-tuple-element.86), channel_id=1, source_target_pairs={{0,1},{1,0},{2,3},{3,2},{4,5},{5,4},{6,7},{7,6},{8,9},{9,8},{10,11... | collective-permute-start | bytes 6152 | tf_op jit(solution)/shard_map/ppermute | solution.py:59
  27.5 2.8 %collective-permute-start.8 = (f32[1,512]{1,0:T(1,128)S(1)}, f32[1,512]{1,0:T(1,128)S(1)}, u32[]{:S(2)}, u32[]{:S(2)}) collective-permute-start(f32[1,512]{1,0:T(1,128)S(1)} %get-tuple-element.87), channel_id=1, source_target_pairs={{0,1},{1,0},{2,3},{3,2},{4,5},{5,4},{6,7},{7,6},{8,9},{9,8},{10,11... | collective-permute-start | bytes 6152 | tf_op jit(solution)/shard_map/ppermute | solution.py:59

commit v4 on v3

--- a/solution.py
+++ b/solution.py
@@ -9,11 +9,15 @@
 
 AXES = ("tm", "col")
 LANES = 128
-MERGE = 3
-JOINS = {2: (0,), 4: (1, 2, 3)}
-VIAS = (-1, 0)
-AHEAD = 7
-STAGES = (6, 8, 10)
+MERGES = {2: ((0, None), (2, 0)), 3: ((0, None), (1, -2))}
+JOINS = {
+    1: ((0,), ()),
+    2: ((1,), ()),
+    3: ((2,), (0, 1)),
+    4: ((3,), (2,)),
+}
+AHEAD = (0, 1, 4, 6, 8, 7, 6)
+STAGES = (6, 10)
 VMEM = pl.BlockSpec(memory_space=pltpu.VMEM)
 FAR = pl.BlockSpec(memory_space=pltpu.HBM)
 
@@ -23,13 +27,17 @@
 
 
 def first_factors(segment, steps):
-    wanted = 3 * segment - 3 + (segment == 1)
-    return smaller(smaller(wanted, AHEAD), steps - 1)
+    wanted = AHEAD[-1]
+    for place in range(len(AHEAD) - 1):
+        if isinstance(segment, int):
+            wanted = AHEAD[place] if segment == place else wanted
+        else:
+            wanted = jnp.where(segment == place, AHEAD[place], wanted)
+    return smaller(wanted, steps - 1)
 
 
 def factors(segment, steps):
-    windows = segment - (segment == 1)
-    return smaller(first_factors(segment, steps) + windows, steps - 1)
+    return smaller(first_factors(segment, steps) + segment - 1, steps - 1)
 
 
 def swap_routes(size, moved):
@@ -52,16 +60,12 @@
         if via is None:
             moved[there] = here ^ 1 if segment + 2 == segments and parts % 2 == 0 else here
         else:
-            moved[there] = via * parts + part
-            moved[via * parts + part] = here
+            middle = via * parts + (part ^ twist)
+            moved[there] = middle
+            moved[middle] = here
         for other in joined:
             moved[other * parts + part] = other * parts + (part ^ 2)
     return lax.ppermute(block, AXES, swap_routes(segments * parts, moved))
-
-
-def swap_parts(block):
-    parts = lax.axis_size("col")
-    return lax.ppermute(block, "col", [(i, i ^ 1) for i in range(parts)])
 
 
 def reduce_rows(total):
@@ -156,16 +160,16 @@
     del jac_in, whole_in, offset_in, rows_in, offs_in
     steps = jac.shape[0]
     segment = lax.axis_index("tm")
-    t = first_factors(segment, steps) + window + 1
+    t = first_factors(segment, steps) + window
     bounds = stage_bounds(steps)
-    late = range(*bounds[window + 1 : window + 3]) if window < 2 else ()
+    late = range(*bounds[1:3]) if window == 1 else ()
 
     @pl.when(segment == 1)
     def _():
         for place in late:
             jac_copy(jac_far, jac, sems, place).start()
 
-    @pl.when(jnp.logical_and(segment > max(window, 1), t < steps))
+    @pl.when(jnp.logical_and(segment > window, t < steps))
     def _():
         offset[...] = add_factor(t, jac, inc, whole, rows, offs, offset[...])
 
@@ -175,7 +179,7 @@
             jac_copy(jac_far, jac, sems, place).wait()
 
 
-def first_kernel(jac_far, inc_far, own_far, jac, inc, sent, whole, offset, rows, offs, own, sems):
+def first_kernel(jac_far, inc_far, own_far, jac, inc, out, kept, whole, offset, rows, offs, own, sems):
     steps, order, _ = jac.shape
     width = own.shape[1]
     segment = lax.axis_index("tm")
@@ -210,13 +214,13 @@
         vector = jnp.concatenate(
             [jnp.where(index == place, block, zero) for place in range(order // width)], axis=1
         )
-        sent[:, order:] = vector
+        kept[...] = vector
 
         def body(t, current):
             arrived(t)
             return step(jac, inc, t, current, index == 0)
 
-        sent[:, :order] = lax.fori_loop(0, steps, body, vector)
+        out[...] = lax.fori_loop(0, steps, body, vector)
 
     @pl.when(segment > 0)
     def _():
@@ -241,11 +245,12 @@
         lax.fori_loop(1 + count, now, finish, 0)
 
 
-def join_kernel(mine, theirs, out, kept):
-    order = out.shape[1]
-    total = mine[...] + theirs[...]
-    out[...] = total[:, :order]
-    kept[...] = total[:, order:]
+def leading(k):
+    added = sum(
+        twist for segment, turns in MERGES.items() if segment < k for twist, _ in turns
+    )
+    missing = lax.axis_size("col") - 1 - added
+    return (lax.axis_index("col") & missing) == 0 if missing else None
 
 
 def hop_kernel(k, joined, far, inc, whole, offset, kept, *refs):
@@ -256,7 +261,7 @@
         received, (out, start) = refs[1:-2], refs[-2:]
     here = lax.axis_index("tm") == k
     steps = jac.shape[0]
-    late = stage_bounds(steps)[3] if far else steps
+    late = stage_bounds(steps)[2] if far else steps
 
     @pl.when(here)
     def _():
@@ -266,7 +271,7 @@
         for other in received[1:]:
             vector = vector + other[...]
         start[...] = vector
-        keep = lax.axis_index("col") < 2 if k <= MERGE else None
+        keep = leading(k)
         done = 1 + factors(k, steps)
         vector = apply_whole(whole, masked(keep, offset[...]), vector)
         if done < late:
@@ -350,12 +355,13 @@
         pltpu.with_memory_space_constraint(array, pltpu.HBM)
         for array in (jacobians, increments, initial[None, :])
     ]
-    jac, inc, sent, whole, offset, rows, offs = call(
+    jac, inc, out, kept, whole, offset, rows, offs = call(
         first_kernel,
         (
             pltpu.VMEM(jacobians.shape, f32),
             pltpu.VMEM(increments.shape, f32),
-            pltpu.VMEM((1, 2 * order), f32),
+            row,
+            row,
             pltpu.VMEM((order, order), f32),
             row,
             pltpu.VMEM((steps, width, order), f32),
@@ -370,7 +376,7 @@
 
     def more(window):
         if window > 1 and all(
-            first_factors(segment, steps) + window >= steps - 1
+            first_factors(segment, steps) + window >= steps
             for segment in range(window + 1, segments)
         ):
             return near
@@ -391,19 +397,14 @@
         )
         return [jac, inc, *rest]
 
-    theirs = swap_parts(sent)
-    near = more(0)
-    out, kept = call(join_kernel, (row, row), sent, theirs)
     last = segments - 1
     for k in range(1, segments):
-        joined = JOINS.get(k - 1, ())
-        if k == MERGE + 1:
-            received = [
-                hop(out, MERGE, 2 * twist, VIAS[twist] % segments, joined)
-                for twist in range(parts // 2)
-            ]
-        else:
-            received = [hop(out, k - 1, joined=joined)]
+        near_joins, far_joins = JOINS.get(k - 1, ((), ()))
+        joined = near_joins + far_joins
+        received = [
+            hop(out, k - 1, twist, None if via is None else via % segments, far_joins)
+            for twist, via in MERGES.get(k - 1, ((0, None),))
+        ]
         near = more(k)
         jac, inc, whole, offset, rows, offs = near
         if k < last:

time: 30.5 us -> 29.5 us (0.967)
  the two profiles are of different devices: /device:TPU:11 before, /device:TPU:24 now
where the time goes in v4:
time: 29.5 us; the launch traced here: 29.4 us
  Pallas kernels  15.2 us (52%)
  starting transfers between devices  10.4 us (35%)
  waiting for transfers between devices  3.65 us (12%)
    pallas_call x14, Pallas kernels, call(): pl.pallas_call(kernel, out_shape=outs, in_specs=[FAR if place in far else...  15.2 us
    ppermute x9, starting transfers between devices, hop(): return lax.ppermute(block, AXES, swap_routes(segments * parts, moved))  10.4 us
    ppermute x9, waiting for transfers between devices, hop(): return lax.ppermute(block, AXES, swap_routes(segments * parts, moved))  3.65 us
  transfers between devices with their start and end apart: 9, of which 2 were waited for; matrix products, arithmetic and copies ran while one was open for 0% of the time, Pallas kernels for 23%

profile of v4, /device:TPU:24, one launch (start us, length us, event | category | flops | bytes accessed | tf_op | source)
XLA Modules:
  0.0 29.4 jit_solution(5135775768521024056)
XLA Ops:
  0.0 8.0 %shard_map.37 = (f32[12,512,512]{2,1,0:T(8,128)S(1)}, f32[12,512]{1,0:T(8,128)S(1)}, f32[1,512]{1,0:T(1,128)S(1)}, f32[1,512]{1,0:T(1,128)S(1)}, f32[512,512]{1,...) custom-call(f32[12,512,512]{2,1,0:T(8,128)} %jac_far.11, ...), custom_call_target="tpu_custom_call" | custom-call | tf_op jit(solution)/shard_map/pallas_call | solution.py:336
  8.1 0.1 collective-permute-start
  8.1 1.2 %shard_map.38 = (f32[12,512,512]{2,1,0:T(8,128)S(1)}, f32[512,512]{1,0:T(8,128)S(1)}, f32[1,512]{1,0:T(1,128)S(1)}, f32[12,128,512]{2,1,0:T(8,128)S(1)}, f32[12,128]{1,0:T(8,128)S(1)}) custom-call(f32[12,512,512]{2,1,0:T(8,128)} %jac_far.11, ...), custom_call_target="tpu_custom_call", output_to_operand_aliasing={{0}: (1, {}), {1}: (3, {}), {2}: (4, {}), {3}: (5, {}), {4}... | custom-call | flops 268435456 | bytes 268435456 | tf_op jit(solution)/shard_map/pallas_call | solution.py:336
  9.3 0.0 collective-permute-done.refs_2_
  9.3 0.1 shard_map.39
  9.5 0.5 %collective-permute-start.1 = (f32[1,512]{1,0:T(1,128)S(1)}, f32[1,512]{1,0:T(1,128)S(1)}, u32[]{:S(2)}, u32[]{:S(2)}) collective-permute-start(f32[1,512]{1,0:T(1,128)S(1)} %get-tuple-element.86), channel_id=1, source_target_pairs={{0,1},{1,0},{2,3},{3,2},{4,8},{5,9},{6,10},{7,11},{8,4},{9,5},{10,... | collective-permute-start | bytes 6152 | tf_op jit(solution)/shard_map/ppermute | solution.py:68
  10.0 1.1 %shard_map.40 = (f32[12,512,512]{2,1,0:T(8,128)S(1)}, f32[512,512]{1,0:T(8,128)S(1)}, f32[1,512]{1,0:T(1,128)S(1)}, f32[12,128,512]{2,1,0:T(8,128)S(1)}, f32[12,128]{1,0:T(8,128)S(1)}) custom-call(f32[12,512,512]{2,1,0:T(8,128)} %jac_far.11, ...), custom_call_target="tpu_custom_call", output_to_operand_aliasing={{0}: (1, {}), {1}: (3, {}), {2}: (4, {}), {3}: (5, {}), {4}... | custom-call | flops 268435456 | bytes 268435456 | tf_op jit(solution)/shard_map/pallas_call | solution.py:336
  11.2 0.0 collective-permute-done.1.refs_1_
  11.2 0.1 collective-permute-start.3
  11.3 0.5 %collective-permute-start.2 = (f32[1,512]{1,0:T(1,128)S(1)}, f32[1,512]{1,0:T(1,128)S(1)}, u32[]{:S(2)}, u32[]{:S(2)}) collective-permute-start(f32[1,512]{1,0:T(1,128)S(1)} %get-tuple-element.88), channel_id=1, source_target_pairs={{0,1},{1,0},{2,3},{3,2},{4,5},{5,4},{6,7},{7,6},{8,12},{9,13},{10,... | collective-permute-start | bytes 6152 | tf_op jit(solution)/shard_map/ppermute | solution.py:68
  11.7 1.1 %shard_map.41 = (f32[12,512,512]{2,1,0:T(8,128)S(1)}, f32[512,512]{1,0:T(8,128)S(1)}, f32[1,512]{1,0:T(1,128)S(1)}, f32[12,128,512]{2,1,0:T(8,128)S(1)}, f32[12,128]{1,0:T(8,128)S(1)}) custom-call(f32[12,512,512]{2,1,0:T(8,128)} %jac_far.11, ...), custom_call_target="tpu_custom_call", output_to_operand_aliasing={{0}: (1, {}), {1}: (3, {}), {2}: (4, {}), {3}: (5, {}), {4}... | custom-call | flops 268435456 | bytes 268435456 | tf_op jit(solution)/shard_map/pallas_call | solution.py:336
  12.9 0.0 collective-permute-done.3.refs_2_
  12.9 0.0 collective-permute-done.2.refs_1_
  13.0 3.3 %collective-permute-start.5 = (f32[1,512]{1,0:T(1,128)S(1)}, f32[1,512]{1,0:T(1,128)S(1)}, u32[]{:S(2)}, u32[]{:S(2)}) collective-permute-start(f32[1,512]{1,0:T(1,128)S(1)} %get-tuple-element.90), channel_id=1, source_target_pairs={{0,2},{1,3},{2,0},{3,1},{4,6},{5,7},{6,4},{7,5},{8,9},{9,8},{10,11... | collective-permute-start | bytes 6152 | tf_op jit(solution)/shard_map/ppermute | solution.py:68
  16.3 2.7 %collective-permute-start.4 = (f32[1,512]{1,0:T(1,128)S(1)}, f32[1,512]{1,0:T(1,128)S(1)}, u32[]{:S(2)}, u32[]{:S(2)}) collective-permute-start(f32[1,512]{1,0:T(1,128)S(1)} %get-tuple-element.90), channel_id=1, source_target_pairs={{0,2},{1,3},{2,0},{3,1},{4,6},{5,7},{6,4},{7,5},{8,9},{9,8},{10,11... | collective-permute-start | bytes 6152 | tf_op jit(solution)/shard_map/ppermute | solution.py:68
  19.0 1.1 %shard_map.42 = (f32[12,512,512]{2,1,0:T(8,128)S(1)}, f32[512,512]{1,0:T(8,128)S(1)}, f32[1,512]{1,0:T(1,128)S(1)}, f32[12,128,512]{2,1,0:T(8,128)S(1)}, f32[12,128]{1,0:T(8,128)S(1)}) custom-call(f32[12,512,512]{2,1,0:T(8,128)} %jac_far.11, ...), custom_call_target="tpu_custom_call", output_to_operand_aliasing={{0}: (1, {}), {1}: (3, {}), {2}: (4, {}), {3}: (5, {}), {4}... | custom-call | flops 268435456 | bytes 268435456 | tf_op jit(solution)/shard_map/pallas_call | solution.py:336
  20.2 0.1 collective-permute-start.6
  20.3 1.2 %shard_map.43 = (f32[12,512,512]{2,1,0:T(8,128)S(1)}, f32[512,512]{1,0:T(8,128)S(1)}, f32[1,512]{1,0:T(1,128)S(1)}, f32[12,128,512]{2,1,0:T(8,128)S(1)}, f32[12,128]{1,0:T(8,128)S(1)}) custom-call(f32[12,512,512]{2,1,0:T(8,128)} %jac_far.11, ...), custom_call_target="tpu_custom_call", output_to_operand_aliasing={{0}: (1, {}), {1}: (3, {}), {2}: (4, {}), {3}: (5, {}), {4}... | custom-call | flops 268435456 | bytes 268435456 | tf_op jit(solution)/shard_map/pallas_call | solution.py:336
  21.5 3.1 %collective-permute-start.7 = (f32[1,512]{1,0:T(1,128)S(1)}, f32[1,512]{1,0:T(1,128)S(1)}, u32[]{:S(2)}, u32[]{:S(2)}) collective-permute-start(f32[1,512]{1,0:T(1,128)S(1)} %get-tuple-element.94), channel_id=1, source_target_pairs={{0,1},{1,0},{2,3},{3,2},{4,5},{5,4},{6,7},{7,6},{8,9},{9,8},{10,11... | collective-permute-start | bytes 6152 | tf_op jit(solution)/shard_map/ppermute | solution.py:68
  24.6 1.6 %collective-permute-done.7.refs_1_ = f32[1,512]{1,0:T(1,128)S(1)} collective-permute-done((f32[1,512]{1,0:T(1,128)S(1)}, f32[1,512]{1,0:T(1,128)S(1)}, u32[]{:S(2)}, u32[]{:S(2)}) %collective-permute-start.7) | collective-permute-done | bytes 2080 | tf_op jit(solution)/shard_map/ppermute | solution.py:68
  26.1 0.2 shard_map.48
  26.3 0.1 collective-permute-start.8
  26.4 0.9 %shard_map.49.before = f32[12,128]{1,0:T(8,128)} custom-call(f32[12,512,512]{2,1,0:T(8,128)S(1)} %get-tuple-element.80.refs_0_.jac, f32[12,512]{1,0:T(8,128)S(1)} %get-tuple-element.51.inc, f32[12,128,512]{2,1,0:T(8,128)S(1)} %get-tuple-element.81.rows, f32[12,128]{1,0:T(8,128)S(1)} %get-tuple-element.82.offs, f32[1,512]{1,0:T(1,128)S(1)} %get-tuple-element.96.kept), custom_call_target="tpu_custom_call" | custom-call | flops 12582912 | bytes 12582912 | tf_op jit(solution)/shard_map/pallas_call | solution.py:336
  27.3 2.1 %collective-permute-done.8.received = f32[1,512]{1,0:T(1,128)S(1)} collective-permute-done((f32[1,512]{1,0:T(1,128)S(1)}, f32[1,512]{1,0:T(1,128)S(1)}, u32[]{:S(2)}, u32[]{:S(2)}) %collective-permute-start.8) | collective-permute-done | bytes 2080 | tf_op jit(solution)/shard_map/ppermute | solution.py:68
  (8 shorter events, 0.1 us)
Async XLA Ops:
  8.1 1.3 %collective-permute-start = (f32[1,512]{1,0:T(1,128)S(1)}, f32[1,512]{1,0:T(1,128)S(1)}, u32[]{:S(2)}, u32[]{:S(2)}) collective-permute-start(f32[1,512]{1,0:T(1,128)S(1)} %get-tuple-element.61), channel_id=1, source_target_pairs={{0,4},{1,5},{2,6},{3,7},{4,0},{5,1},{6,2},{7,3},{8,9},{9,8},{10,11... | collective-permute-start | bytes 6152 | tf_op jit(solution)/shard_map/ppermute | solution.py:68
  9.5 1.7 %collective-permute-start.1 = (f32[1,512]{1,0:T(1,128)S(1)}, f32[1,512]{1,0:T(1,128)S(1)}, u32[]{:S(2)}, u32[]{:S(2)}) collective-permute-start(f32[1,512]{1,0:T(1,128)S(1)} %get-tuple-element.86), channel_id=1, source_target_pairs={{0,1},{1,0},{2,3},{3,2},{4,8},{5,9},{6,10},{7,11},{8,4},{9,5},{10,... | collective-permute-start | bytes 6152 | tf_op jit(solution)/shard_map/ppermute | solution.py:68
  11.2 1.7 %collective-permute-start.3 = (f32[1,512]{1,0:T(1,128)S(1)}, f32[1,512]{1,0:T(1,128)S(1)}, u32[]{:S(2)}, u32[]{:S(2)}) collective-permute-start(f32[1,512]{1,0:T(1,128)S(1)} %get-tuple-element.88), channel_id=1, source_target_pairs={{0,10},{1,11},{2,8},{3,9},{4,5},{5,4},{6,7},{7,6},{8,14},{9,15},{1... | collective-permute-start | bytes 6152 | tf_op jit(solution)/shard_map/ppermute | solution.py:68
  11.3 1.6 %collective-permute-start.2 = (f32[1,512]{1,0:T(1,128)S(1)}, f32[1,512]{1,0:T(1,128)S(1)}, u32[]{:S(2)}, u32[]{:S(2)}) collective-permute-start(f32[1,512]{1,0:T(1,128)S(1)} %get-tuple-element.88), channel_id=1, source_target_pairs={{0,1},{1,0},{2,3},{3,2},{4,5},{5,4},{6,7},{7,6},{8,12},{9,13},{10,... | collective-permute-start | bytes 6152 | tf_op jit(solution)/shard_map/ppermute | solution.py:68
  13.0 7.2 %collective-permute-start.5 = (f32[1,512]{1,0:T(1,128)S(1)}, f32[1,512]{1,0:T(1,128)S(1)}, u32[]{:S(2)}, u32[]{:S(2)}) collective-permute-start(f32[1,512]{1,0:T(1,128)S(1)} %get-tuple-element.90), channel_id=1, source_target_pairs={{0,2},{1,3},{2,0},{3,1},{4,6},{5,7},{6,4},{7,5},{8,9},{9,8},{10,11... | collective-permute-start | bytes 6152 | tf_op jit(solution)/shard_map/ppermute | solution.py:68
  16.3 3.9 %collective-permute-start.4 = (f32[1,512]{1,0:T(1,128)S(1)}, f32[1,512]{1,0:T(1,128)S(1)}, u32[]{:S(2)}, u32[]{:S(2)}) collective-permute-start(f32[1,512]{1,0:T(1,128)S(1)} %get-tuple-element.90), channel_id=1, source_target_pairs={{0,2},{1,3},{2,0},{3,1},{4,6},{5,7},{6,4},{7,5},{8,9},{9,8},{10,11... | collective-permute-start | bytes 6152 | tf_op jit(solution)/shard_map/ppermute | solution.py:68
  20.2 1.3 %collective-permute-start.6 = (f32[1,512]{1,0:T(1,128)S(1)}, f32[1,512]{1,0:T(1,128)S(1)}, u32[]{:S(2)}, u32[]{:S(2)}) collective-permute-start(f32[1,512]{1,0:T(1,128)S(1)} %get-tuple-element.92), channel_id=1, source_target_pairs={{0,1},{1,0},{2,3},{3,2},{4,5},{5,4},{6,7},{7,6},{8,10},{9,11},{10,... | collective-permute-start | bytes 6152 | tf_op jit(solution)/shard_map/ppermute | solution.py:68
  21.5 4.6 %collective-permute-start.7 = (f32[1,512]{1,0:T(1,128)S(1)}, f32[1,512]{1,0:T(1,128)S(1)}, u32[]{:S(2)}, u32[]{:S(2)}) collective-permute-start(f32[1,512]{1,0:T(1,128)S(1)} %get-tuple-element.94), channel_id=1, source_target_pairs={{0,1},{1,0},{2,3},{3,2},{4,5},{5,4},{6,7},{7,6},{8,9},{9,8},{10,11... | collective-permute-start | bytes 6152 | tf_op jit(solution)/shard_map/ppermute | solution.py:68
  26.3 3.1 %collective-permute-start.8 = (f32[1,512]{1,0:T(1,128)S(1)}, f32[1,512]{1,0:T(1,128)S(1)}, u32[]{:S(2)}, u32[]{:S(2)}) collective-permute-start(f32[1,512]{1,0:T(1,128)S(1)} %get-tuple-element.95), channel_id=1, source_target_pairs={{0,1},{1,0},{2,3},{3,2},{4,5},{5,4},{6,7},{7,6},{8,9},{9,8},{10,11... | collective-permute-start | bytes 6152 | tf_op jit(solution)/shard_map/ppermute | solution.py:68

commit v5 on v4

--- a/solution.py
+++ b/solution.py
@@ -16,8 +16,8 @@
     3: ((2,), (0, 1)),
     4: ((3,), (2,)),
 }
-AHEAD = (0, 1, 4, 6, 8, 7, 6)
-STAGES = (6, 10)
+AHEAD = (0, 2, 4, 6, 8, 7, 6)
+STAGES = (8, 10)
 VMEM = pl.BlockSpec(memory_space=pltpu.VMEM)
 FAR = pl.BlockSpec(memory_space=pltpu.HBM)
 

time: 29.5 us -> 29.2 us (0.990)
  starting transfers between devices: 10.4 us -> 10 us
    ppermute x9, starting transfers between devices: 10.4 us -> 10 us  [hop(): return lax.ppermute(block, AXES, swap_routes(segments * parts, moved))]
where the time goes in v5:
time: 29.2 us; the launch traced here: 29 us
  Pallas kernels  15.1 us (52%)
  starting transfers between devices  10 us (34%)
  waiting for transfers between devices  3.65 us (12%)
    pallas_call x14, Pallas kernels, call(): pl.pallas_call(kernel, out_shape=outs, in_specs=[FAR if place in far else...  15.1 us
    ppermute x9, starting transfers between devices, hop(): return lax.ppermute(block, AXES, swap_routes(segments * parts, moved))  10 us
    ppermute x9, waiting for transfers between devices, hop(): return lax.ppermute(block, AXES, swap_routes(segments * parts, moved))  3.65 us
  transfers between devices with their start and end apart: 9, of which 2 were waited for; matrix products, arithmetic and copies ran while one was open for 0% of the time, Pallas kernels for 23%

profile of v5, /device:TPU:24, one launch (start us, length us, event | category | flops | bytes accessed | tf_op | source)
XLA Modules:
  0.0 29.0 jit_solution(2702227859808372591)
XLA Ops:
  0.0 8.0 %shard_map.37 = (f32[12,512,512]{2,1,0:T(8,128)S(1)}, f32[12,512]{1,0:T(8,128)S(1)}, f32[1,512]{1,0:T(1,128)S(1)}, f32[1,512]{1,0:T(1,128)S(1)}, f32[512,512]{1,...) custom-call(f32[12,512,512]{2,1,0:T(8,128)} %jac_far.11, ...), custom_call_target="tpu_custom_call" | custom-call | tf_op jit(solution)/shard_map/pallas_call | solution.py:336
  8.1 0.1 collective-permute-start
  8.1 1.2 %shard_map.38 = (f32[12,512,512]{2,1,0:T(8,128)S(1)}, f32[512,512]{1,0:T(8,128)S(1)}, f32[1,512]{1,0:T(1,128)S(1)}, f32[12,128,512]{2,1,0:T(8,128)S(1)}, f32[12,128]{1,0:T(8,128)S(1)}) custom-call(f32[12,512,512]{2,1,0:T(8,128)} %jac_far.11, ...), custom_call_target="tpu_custom_call", output_to_operand_aliasing={{0}: (1, {}), {1}: (3, {}), {2}: (4, {}), {3}: (5, {}), {4}... | custom-call | flops 268435456 | bytes 268435456 | tf_op jit(solution)/shard_map/pallas_call | solution.py:336
  9.3 0.1 shard_map.39
  9.5 0.5 %collective-permute-start.1 = (f32[1,512]{1,0:T(1,128)S(1)}, f32[1,512]{1,0:T(1,128)S(1)}, u32[]{:S(2)}, u32[]{:S(2)}) collective-permute-start(f32[1,512]{1,0:T(1,128)S(1)} %get-tuple-element.86), channel_id=1, source_target_pairs={{0,1},{1,0},{2,3},{3,2},{4,8},{5,9},{6,10},{7,11},{8,4},{9,5},{10,... | collective-permute-start | bytes 6152 | tf_op jit(solution)/shard_map/ppermute | solution.py:68
  10.0 1.1 %shard_map.40 = (f32[12,512,512]{2,1,0:T(8,128)S(1)}, f32[512,512]{1,0:T(8,128)S(1)}, f32[1,512]{1,0:T(1,128)S(1)}, f32[12,128,512]{2,1,0:T(8,128)S(1)}, f32[12,128]{1,0:T(8,128)S(1)}) custom-call(f32[12,512,512]{2,1,0:T(8,128)} %jac_far.11, ...), custom_call_target="tpu_custom_call", output_to_operand_aliasing={{0}: (1, {}), {1}: (3, {}), {2}: (4, {}), {3}: (5, {}), {4}... | custom-call | flops 268435456 | bytes 268435456 | tf_op jit(solution)/shard_map/pallas_call | solution.py:336
  11.2 0.0 collective-permute-done.1.refs_1_
  11.2 0.1 collective-permute-start.3
  11.3 0.5 %collective-permute-start.2 = (f32[1,512]{1,0:T(1,128)S(1)}, f32[1,512]{1,0:T(1,128)S(1)}, u32[]{:S(2)}, u32[]{:S(2)}) collective-permute-start(f32[1,512]{1,0:T(1,128)S(1)} %get-tuple-element.88), channel_id=1, source_target_pairs={{0,1},{1,0},{2,3},{3,2},{4,5},{5,4},{6,7},{7,6},{8,12},{9,13},{10,... | collective-permute-start | bytes 6152 | tf_op jit(solution)/shard_map/ppermute | solution.py:68
  11.7 1.1 %shard_map.41 = (f32[12,512,512]{2,1,0:T(8,128)S(1)}, f32[512,512]{1,0:T(8,128)S(1)}, f32[1,512]{1,0:T(1,128)S(1)}, f32[12,128,512]{2,1,0:T(8,128)S(1)}, f32[12,128]{1,0:T(8,128)S(1)}) custom-call(f32[12,512,512]{2,1,0:T(8,128)} %jac_far.11, ...), custom_call_target="tpu_custom_call", output_to_operand_aliasing={{0}: (1, {}), {1}: (3, {}), {2}: (4, {}), {3}: (5, {}), {4}... | custom-call | flops 268435456 | bytes 268435456 | tf_op jit(solution)/shard_map/pallas_call | solution.py:336
  12.9 0.0 collective-permute-done.3.refs_2_
  12.9 0.0 collective-permute-done.2.refs_1_
  13.0 3.3 %collective-permute-start.5 = (f32[1,512]{1,0:T(1,128)S(1)}, f32[1,512]{1,0:T(1,128)S(1)}, u32[]{:S(2)}, u32[]{:S(2)}) collective-permute-start(f32[1,512]{1,0:T(1,128)S(1)} %get-tuple-element.90), channel_id=1, source_target_pairs={{0,2},{1,3},{2,0},{3,1},{4,6},{5,7},{6,4},{7,5},{8,9},{9,8},{10,11... | collective-permute-start | bytes 6152 | tf_op jit(solution)/shard_map/ppermute | solution.py:68
  16.3 2.3 %collective-permute-start.4 = (f32[1,512]{1,0:T(1,128)S(1)}, f32[1,512]{1,0:T(1,128)S(1)}, u32[]{:S(2)}, u32[]{:S(2)}) collective-permute-start(f32[1,512]{1,0:T(1,128)S(1)} %get-tuple-element.90), channel_id=1, source_target_pairs={{0,2},{1,3},{2,0},{3,1},{4,6},{5,7},{6,4},{7,5},{8,9},{9,8},{10,11... | collective-permute-start | bytes 6152 | tf_op jit(solution)/shard_map/ppermute | solution.py:68
  18.6 1.1 %shard_map.42 = (f32[12,512,512]{2,1,0:T(8,128)S(1)}, f32[512,512]{1,0:T(8,128)S(1)}, f32[1,512]{1,0:T(1,128)S(1)}, f32[12,128,512]{2,1,0:T(8,128)S(1)}, f32[12,128]{1,0:T(8,128)S(1)}) custom-call(f32[12,512,512]{2,1,0:T(8,128)} %jac_far.11, ...), custom_call_target="tpu_custom_call", output_to_operand_aliasing={{0}: (1, {}), {1}: (3, {}), {2}: (4, {}), {3}: (5, {}), {4}... | custom-call | flops 268435456 | bytes 268435456 | tf_op jit(solution)/shard_map/pallas_call | solution.py:336
  19.8 0.0 collective-permute-done.4.refs_1_
  19.8 0.1 collective-permute-start.6
  19.9 1.2 %shard_map.43 = (f32[12,512,512]{2,1,0:T(8,128)S(1)}, f32[512,512]{1,0:T(8,128)S(1)}, f32[1,512]{1,0:T(1,128)S(1)}, f32[12,128,512]{2,1,0:T(8,128)S(1)}, f32[12,128]{1,0:T(8,128)S(1)}) custom-call(f32[12,512,512]{2,1,0:T(8,128)} %jac_far.11, ...), custom_call_target="tpu_custom_call", output_to_operand_aliasing={{0}: (1, {}), {1}: (3, {}), {2}: (4, {}), {3}: (5, {}), {4}... | custom-call | flops 268435456 | bytes 268435456 | tf_op jit(solution)/shard_map/pallas_call | solution.py:336
  21.1 3.1 %collective-permute-start.7 = (f32[1,512]{1,0:T(1,128)S(1)}, f32[1,512]{1,0:T(1,128)S(1)}, u32[]{:S(2)}, u32[]{:S(2)}) collective-permute-start(f32[1,512]{1,0:T(1,128)S(1)} %get-tuple-element.94), channel_id=1, source_target_pairs={{0,1},{1,0},{2,3},{3,2},{4,5},{5,4},{6,7},{7,6},{8,9},{9,8},{10,11... | collective-permute-start | bytes 6152 | tf_op jit(solution)/shard_map/ppermute | solution.py:68
  24.2 1.6 %collective-permute-done.7.refs_1_ = f32[1,512]{1,0:T(1,128)S(1)} collective-permute-done((f32[1,512]{1,0:T(1,128)S(1)}, f32[1,512]{1,0:T(1,128)S(1)}, u32[]{:S(2)}, u32[]{:S(2)}) %collective-permute-start.7) | collective-permute-done | bytes 2080 | tf_op jit(solution)/shard_map/ppermute | solution.py:68
  25.8 0.2 shard_map.48
  25.9 0.1 collective-permute-start.8
  26.0 0.9 %shard_map.49.before = f32[12,128]{1,0:T(8,128)} custom-call(f32[12,512,512]{2,1,0:T(8,128)S(1)} %get-tuple-element.80.refs_0_.jac, f32[12,512]{1,0:T(8,128)S(1)} %get-tuple-element.51.inc, f32[12,128,512]{2,1,0:T(8,128)S(1)} %get-tuple-element.81.rows, f32[12,128]{1,0:T(8,128)S(1)} %get-tuple-element.82.offs, f32[1,512]{1,0:T(1,128)S(1)} %get-tuple-element.96.kept), custom_call_target="tpu_custom_call" | custom-call | flops 12582912 | bytes 12582912 | tf_op jit(solution)/shard_map/pallas_call | solution.py:336
  27.0 2.1 %collective-permute-done.8.received = f32[1,512]{1,0:T(1,128)S(1)} collective-permute-done((f32[1,512]{1,0:T(1,128)S(1)}, f32[1,512]{1,0:T(1,128)S(1)}, u32[]{:S(2)}, u32[]{:S(2)}) %collective-permute-start.8) | collective-permute-done | bytes 2080 | tf_op jit(solution)/shard_map/ppermute | solution.py:68
  (8 shorter events, 0.1 us)
Async XLA Ops:
  8.1 1.3 %collective-permute-start = (f32[1,512]{1,0:T(1,128)S(1)}, f32[1,512]{1,0:T(1,128)S(1)}, u32[]{:S(2)}, u32[]{:S(2)}) collective-permute-start(f32[1,512]{1,0:T(1,128)S(1)} %get-tuple-element.61), channel_id=1, source_target_pairs={{0,4},{1,5},{2,6},{3,7},{4,0},{5,1},{6,2},{7,3},{8,9},{9,8},{10,11... | collective-permute-start | bytes 6152 | tf_op jit(solution)/shard_map/ppermute | solution.py:68
  9.5 1.7 %collective-permute-start.1 = (f32[1,512]{1,0:T(1,128)S(1)}, f32[1,512]{1,0:T(1,128)S(1)}, u32[]{:S(2)}, u32[]{:S(2)}) collective-permute-start(f32[1,512]{1,0:T(1,128)S(1)} %get-tuple-element.86), channel_id=1, source_target_pairs={{0,1},{1,0},{2,3},{3,2},{4,8},{5,9},{6,10},{7,11},{8,4},{9,5},{10,... | collective-permute-start | bytes 6152 | tf_op jit(solution)/shard_map/ppermute | solution.py:68
  11.2 1.7 %collective-permute-start.3 = (f32[1,512]{1,0:T(1,128)S(1)}, f32[1,512]{1,0:T(1,128)S(1)}, u32[]{:S(2)}, u32[]{:S(2)}) collective-permute-start(f32[1,512]{1,0:T(1,128)S(1)} %get-tuple-element.88), channel_id=1, source_target_pairs={{0,10},{1,11},{2,8},{3,9},{4,5},{5,4},{6,7},{7,6},{8,14},{9,15},{1... | collective-permute-start | bytes 6152 | tf_op jit(solution)/shard_map/ppermute | solution.py:68
  11.3 1.6 %collective-permute-start.2 = (f32[1,512]{1,0:T(1,128)S(1)}, f32[1,512]{1,0:T(1,128)S(1)}, u32[]{:S(2)}, u32[]{:S(2)}) collective-permute-start(f32[1,512]{1,0:T(1,128)S(1)} %get-tuple-element.88), channel_id=1, source_target_pairs={{0,1},{1,0},{2,3},{3,2},{4,5},{5,4},{6,7},{7,6},{8,12},{9,13},{10,... | collective-permute-start | bytes 6152 | tf_op jit(solution)/shard_map/ppermute | solution.py:68
  13.0 6.8 %collective-permute-start.5 = (f32[1,512]{1,0:T(1,128)S(1)}, f32[1,512]{1,0:T(1,128)S(1)}, u32[]{:S(2)}, u32[]{:S(2)}) collective-permute-start(f32[1,512]{1,0:T(1,128)S(1)} %get-tuple-element.90), channel_id=1, source_target_pairs={{0,2},{1,3},{2,0},{3,1},{4,6},{5,7},{6,4},{7,5},{8,9},{9,8},{10,11... | collective-permute-start | bytes 6152 | tf_op jit(solution)/shard_map/ppermute | solution.py:68
  16.3 3.5 %collective-permute-start.4 = (f32[1,512]{1,0:T(1,128)S(1)}, f32[1,512]{1,0:T(1,128)S(1)}, u32[]{:S(2)}, u32[]{:S(2)}) collective-permute-start(f32[1,512]{1,0:T(1,128)S(1)} %get-tuple-element.90), channel_id=1, source_target_pairs={{0,2},{1,3},{2,0},{3,1},{4,6},{5,7},{6,4},{7,5},{8,9},{9,8},{10,11... | collective-permute-start | bytes 6152 | tf_op jit(solution)/shard_map/ppermute | solution.py:68
  19.8 1.3 %collective-permute-start.6 = (f32[1,512]{1,0:T(1,128)S(1)}, f32[1,512]{1,0:T(1,128)S(1)}, u32[]{:S(2)}, u32[]{:S(2)}) collective-permute-start(f32[1,512]{1,0:T(1,128)S(1)} %get-tuple-element.92), channel_id=1, source_target_pairs={{0,1},{1,0},{2,3},{3,2},{4,5},{5,4},{6,7},{7,6},{8,10},{9,11},{10,... | collective-permute-start | bytes 6152 | tf_op jit(solution)/shard_map/ppermute | solution.py:68
  21.1 4.6 %collective-permute-start.7 = (f32[1,512]{1,0:T(1,128)S(1)}, f32[1,512]{1,0:T(1,128)S(1)}, u32[]{:S(2)}, u32[]{:S(2)}) collective-permute-start(f32[1,512]{1,0:T(1,128)S(1)} %get-tuple-element.94), channel_id=1, source_target_pairs={{0,1},{1,0},{2,3},{3,2},{4,5},{5,4},{6,7},{7,6},{8,9},{9,8},{10,11... | collective-permute-start | bytes 6152 | tf_op jit(solution)/shard_map/ppermute | solution.py:68
  25.9 3.1 %collective-permute-start.8 = (f32[1,512]{1,0:T(1,128)S(1)}, f32[1,512]{1,0:T(1,128)S(1)}, u32[]{:S(2)}, u32[]{:S(2)}) collective-permute-start(f32[1,512]{1,0:T(1,128)S(1)} %get-tuple-element.95), channel_id=1, source_target_pairs={{0,1},{1,0},{2,3},{3,2},{4,5},{5,4},{6,7},{7,6},{8,9},{9,8},{10,11... | collective-permute-start | bytes 6152 | tf_op jit(solution)/shard_map/ppermute | solution.py:68
